TPU v7x, 32 devices: a whole 2x2x4 slice. The times are simulated.
32 devices in a mesh: depth: 4 (over z), row: 2 (over core), col: 4 (over y, x).
Axes of the slice: x: 2, y: 2, z: 4, core: 2. Of those that a mesh axis runs over, the one named last changes fastest.
Arguments:
- volume: bfloat16 [4, 18, 256, 8192], P('depth', None, 'row', 'col'), may hold values from -6 to 6
- order: int32 [4], replicated, may hold values from 0 to 3, each once
- empty: int32 [4, 2, 4], P('depth', 'row', 'col'), may hold values 0 or 1
- bump_center: float32 [4], replicated, may hold values from -1.5 to 1.5
- bump_width: float32 [4], replicated, may hold values from 0.3 to 1
- bump_height: float32 [4], replicated, may hold values from 0.5 to 4
- bump_color: float32 [3, 4], replicated, may hold values from 0.5 to 2
- light_dir: float32 [3], replicated, may hold values from -1 to 1
Outputs:
- image: float32 [2, 4, 128, 8192], P('row', None, 'depth', 'col')
Inputs may be any that keep to these rules, and one draw needn't show every extreme that they name: `order`: a permutation of the depth indices.
All inputs are finite; a program needn't handle non-finite values. No bound on the sum of `empty` on one device may be relied on, other than what follows from the above.
Results may differ from a plain program's by a relative error of at most 0.0003.
Values may be sent and summed in bfloat16 or wider, within the bound.
No kernel may reach another device: no remote copies, remote signals or barrier semaphores. Data moves between devices by JAX's collectives and lax.ppermute only.
A program may use at most 128 MiB of HBM per device.

v0:
```python
import jax
import jax.numpy as jnp
from jax import lax
from jax.sharding import PartitionSpec as P

slab_depth = 8
absorption = 0.08


def with_halo(x, sides, width):
    for axis, dim in sides:
        count, length = (lax.axis_size(axis), x.shape[dim])
        up = [(i, (i + 1) % count) for i in range(count - 1)]
        down = [(j, i) for i, j in up]
        last = lax.slice_in_dim(x, length - width, length, axis=dim)
        leading = lax.slice_in_dim(x, 0, width, axis=dim)
        before = lax.ppermute(last, axis, up)
        after = lax.ppermute(leading, axis, down)
        x = jnp.concatenate([before, x, after], axis=dim)
    return x


def march_brick(padded, bump_center, bump_width, bump_height, bump_color, light_dir):
    depth_len = padded.shape[0] - 2
    row_count = padded.shape[1] - 2
    col_count = padded.shape[2] - 2
    per_sample = absorption / depth_len

    def advance(state_pair, slab_index):
        through, radiance = state_pair
        block_cells = lax.dynamic_slice_in_dim(
            padded, slab_index * slab_depth, slab_depth + 2, 0
        ).astype(jnp.float32)
        samples = block_cells[1:-1, 1:-1, 1:-1]
        grad_z = 0.5 * (block_cells[2:, 1:-1, 1:-1] - block_cells[:-2, 1:-1, 1:-1])
        grad_y = 0.5 * (block_cells[1:-1, 2:, 1:-1] - block_cells[1:-1, :-2, 1:-1])
        grad_x = 0.5 * (block_cells[1:-1, 1:-1, 2:] - block_cells[1:-1, 1:-1, :-2])
        facing = jnp.abs(light_dir[0] * grad_z + light_dir[1] * grad_y + light_dir[2] * grad_x)
        shading = 0.3 + 0.7 * facing / jnp.sqrt(
            grad_z * grad_z + grad_y * grad_y + grad_x * grad_x + 1.0
        )
        density = jnp.zeros_like(samples)
        emission = [jnp.zeros_like(samples) for channel in range(3)]
        for bump_index in range(bump_center.shape[0]):
            offset = samples - bump_center[bump_index]
            bump_value = jnp.exp(
                -offset * offset / (2.0 * bump_width[bump_index] * bump_width[bump_index])
            )
            density = density + bump_height[bump_index] * bump_value
            emission = [
                emission[channel] + bump_color[channel, bump_index] * bump_value
                for channel in range(3)
            ]
        passing = jnp.exp(-per_sample * density)
        inclusive = jnp.cumprod(passing, axis=0)
        transmit = jnp.concatenate([jnp.ones_like(passing[:1]), inclusive[:-1]], 0) * through
        weights = transmit * (1.0 - passing) * shading
        radiance = radiance + jnp.stack(
            [jnp.sum(weights * emission[channel], 0) for channel in range(3)]
        )
        return ((through * inclusive[-1], radiance), None)

    start_carry = (
        jnp.ones((row_count, col_count), jnp.float32),
        jnp.zeros((3, row_count, col_count), jnp.float32),
    )
    (through, radiance), unused = lax.scan(
        advance, start_carry, jnp.arange(depth_len // slab_depth, dtype=jnp.int32)
    )
    return jnp.concatenate([radiance, (1.0 - through)[None]], 0)


def composite(stacked, order):
    ranked = jnp.take(stacked, order, axis=0)

    def layer_over(state_pair, layer_image):
        through, summed = state_pair
        summed = summed + through[None] * layer_image
        return ((through * (1.0 - layer_image[3]), summed), None)

    start_carry = (
        jnp.ones(stacked.shape[2:], jnp.float32),
        jnp.zeros(stacked.shape[1:], jnp.float32),
    )
    (through, summed), unused = lax.scan(layer_over, start_carry, ranked)
    return summed


def per_device(volume, order, empty, bump_center, bump_width, bump_height, bump_color, light_dir):
    padded = with_halo(volume[0], (("row", 1), ("col", 2)), 1)
    row_count = volume.shape[2]
    col_count = volume.shape[3]

    def blank_layer():
        return jnp.zeros((4, row_count, col_count), jnp.float32)

    def lit_layer():
        return march_brick(padded, bump_center, bump_width, bump_height, bump_color, light_dir)

    layer_image = lax.cond(empty[0, 0, 0] == 1, blank_layer, lit_layer)
    band_rows = composite(
        lax.all_to_all(layer_image[None], "depth", split_axis=2, concat_axis=0, tiled=True), order
    )
    return band_rows[None]


def solution(mesh):
    placed = (
        P("depth", None, "row", "col"),
        P(),
        P("depth", "row", "col"),
        P(),
        P(),
        P(),
        P(),
        P(),
    )
    return jax.shard_map(
        per_device,
        mesh=mesh,
        in_specs=placed,
        out_specs=P("row", None, "depth", "col"),
        check_vma=False,
    )
```

profile of v0, /device:TPU:0, one launch (start us, length us, event | category | flops | bytes accessed | tf_op | source)
XLA Modules:
  0.0 430.6 jit_solution(2655064788858189192)
XLA Ops:
  0.0 11.8 %copy.50 = bf16[1,18,128,2048]{3,1,2,0:T(8,128)(2,1)S(1)} copy(bf16[1,18,128,2048]{3,2,1,0:T(8,128)(2,1)} %param.14) | data formatting | bytes 18874368 | tf_op args[0]
  11.8 2.4 collective-permute-start
  14.2 1.3 collective-permute-start.1
  15.5 1.9 collective-permute-done.1
  17.4 3.0 pad_maximum_fusion.1
  20.4 4.6 %copy-done.2 = bf16[18,130,2048]{2,0,1:T(8,128)(2,1)} copy-done((bf16[18,130,2048]{2,0,1:T(8,128)(2,1)}, bf16[18,130,2048]{2,0,1:T(8,128)(2,1)S(1)}, u32[]{:S(2)}) %copy-start.2) | copy-done | bytes 9584664
  24.9 0.4 fusion.18
  25.4 0.7 copy.37
  26.0 4.2 collective-permute-start.2
  30.3 0.7 copy.38
  30.9 1.3 collective-permute-start.3
  32.9 11.0 %copy.40 = bf16[18,130,2048]{2,1,0:T(8,128)(2,1)} copy(bf16[18,130,2048]{2,0,1:T(8,128)(2,1)} %copy-done.2) | data formatting | bytes 19169280 | tf_op jit(solution)/shard_map/concatenate | solution.py:19
  44.3 0.4 copy.41
  44.7 19.2 %concatenate.13 = bf16[18,130,2050]{2,1,0:T(8,128)(2,1)} concatenate(bf16[18,130,1]{2,1,0:T(8,128)(2,1)S(1)} %copy.39, bf16[18,130,2048]{2,1,0:T(8,128)(2,1)} %copy.40, bf16[18,130,1]{2,1,0:T(8,128)(2,1)S(1)} %copy.41), dimensions={2} | concatenate | bytes 19188000 | tf_op jit(solution)/shard_map/concatenate | solution.py:19
  63.9 8.1 %conditional.1 = (f32[4,128,2048]{2,1,0:T(8,128)}) conditional(s32[]{:T(128)} %bitcast.8, (f32[4]{0:T(128)S(1)}, f32[3]{0:T(128)S(1)}, f32[4]{0:T(128)}, bf16[18,130,2050]{2,1,0:T(8,128)(2,1)}, f32[4]{0:T(128)}, /*index=5*/f32[3,4]{1,0:T(4,128)}) %tuple.113, () %tuple.27), branch_computations={%region_0.7_spmd, %region_7.8_spmd} | conditional | flops 264809024 | bytes 243180832 | solution.py:100
  69.6 2.5 broadcast.64
  72.1 6.9 %copy.52 = f32[4,128,2048]{2,0,1:T(4,128)} copy(f32[4,128,2048]{2,1,0:T(8,128)} %get-tuple-element.623) | data formatting | bytes 8388608 | tf_op jit(solution)/shard_map/cond | solution.py:100
  78.9 230.3 %all-to-all-start = ((f32[1,4,128,2048]{3,1,0,2:T(4,128)}), f32[1,4,128,2048]{3,1,0,2:T(4,128)}, u32[]{:S(2)}, u32[]{:S(2)}) async-start(f32[1,4,128,2048]{3,1,0,2:T(4,128)} %bitcast.118), calls=%async_computation | async-start | bytes 8388608 | tf_op jit(solution)/shard_map/all_to_all | solution.py:102
  309.2 93.1 %all-to-all-done = f32[1,4,128,2048]{3,1,0,2:T(4,128)} async-done(((f32[1,4,128,2048]{3,1,0,2:T(4,128)}), f32[1,4,128,2048]{3,1,0,2:T(4,128)}, u32[]{:S(2)}, u32[]{:S(2)}) %all-to-all-start) | async-done | bytes 4194336 | tf_op jit(solution)/shard_map/all_to_all | solution.py:102
  402.4 6.6 %copy.51 = f32[1,4,4,32,2048]{4,3,1,2,0:T(8,128)} copy(f32[1,4,4,32,2048]{4,1,3,2,0:T(4,128)} %bitcast.11) | data formatting | bytes 8388608 | tf_op jit(solution)/shard_map/all_to_all | solution.py:102
  409.0 5.0 %gather_fusion = f32[4,4,32,2048]{3,2,1,0:T(8,128)} fusion(f32[4,4,32,2048]{3,2,1,0:T(8,128)} %bitcast.119, s32[1024]{0:T(1024)S(1)} %pad_clamp_fusion), kind=kCustom, calls=%fused_computation | custom fusion | bytes 8388624 | tf_op jit(solution)/shard_map/jit(_take)/gather | solution.py:74
  413.9 4.9 %broadcast_select_fusion.2 = f32[4,4,32,2048]{3,2,1,0:T(8,128)} fusion(f32[4,4,32,2048]{3,2,1,0:T(8,128)} %gather_fusion, pred[4]{0:T(512)(128)(4,1)S(1)} %compare_and_fusion), kind=kLoop, calls=%fused_computation.39 | loop fusion | flops 1048576 | bytes 8388612 | tf_op jit(solution)/shard_map/jit(_take)/select_n | solution.py:74
  418.8 10.6 %while.28 = (s32[]{:T(128)}, f32[32,2048]{1,0:T(8,128)S(1)}, f32[4,32,2048]{2,1,0:T(8,128)S(1)}, f32[4,4,32,2048]{3,2,1,0:T(8,128)}, s32[]{:T(128)}, /*index=5*/s32[]{:T(128)}, s32[]{}) while((s32[]{:T(128)}, f32[32,2048]{1,0:T(8,128)S(1)}, f32[4,32,2048]{2,1,0:T(8,128)S(1)}, f32[4,4,32,2048]{3,2,1,0:T(8,128)}, s32[]{:T(128)}, ...), condition=%wide.region_9.10_spmd.clone, body=%wide.region_8.9_spmd.clone.sunk | while | flops 983044 | bytes 4456560 | solution.py:85
  418.8 1.0 fusion.26
  419.8 1.6 fusion.27
  421.5 1.0 fusion.26
  422.5 1.6 fusion.27
  424.1 1.0 fusion.26
  425.2 1.6 fusion.27
  426.8 1.0 fusion.26
  427.8 1.6 fusion.27
  429.5 1.0 copy-done.3
  (18 shorter events, 0.4 us)
Async XLA Ops:
  11.8 3.7 collective-permute-start
  14.2 3.2 collective-permute-start.1
  20.3 4.6 %copy-start.2 = (bf16[18,130,2048]{2,0,1:T(8,128)(2,1)}, bf16[18,130,2048]{2,0,1:T(8,128)(2,1)S(1)}, u32[]{:S(2)}) copy-start(bf16[18,130,2048]{2,0,1:T(8,128)(2,1)S(1)} %pad_maximum_fusion.1) | copy-start | bytes 28753924
  26.0 17.8 %collective-permute-start.2 = (bf16[18,130,1]{1,0,2:T(8,128)(2,1)S(1)}, bf16[18,130,1]{1,0,2:T(8,128)(2,1)S(1)}, u32[]{:S(2)}, u32[]{:S(2)}) collective-permute-start(bf16[18,130,1]{1,0,2:T(8,128)(2,1)S(1)} %copy.37), channel_id=1, source_target_pairs={{0,1},{1,2},{2,3},{4,5},{5,6},{6,7},{8,9},{9,10},{10,11},{12,13},{... | collective-permute-start | bytes 14048 | tf_op jit(solution)/shard_map/ppermute | solution.py:17
  30.9 13.3 %collective-permute-start.3 = (bf16[18,130,1]{1,0,2:T(8,128)(2,1)S(1)}, bf16[18,130,1]{1,0,2:T(8,128)(2,1)S(1)}, u32[]{:S(2)}, u32[]{:S(2)}) collective-permute-start(bf16[18,130,1]{1,0,2:T(8,128)(2,1)S(1)} %copy.38), channel_id=1, source_target_pairs={{1,0},{2,1},{3,2},{5,4},{6,5},{7,6},{9,8},{10,9},{11,10},{13,12},{... | collective-permute-start | bytes 14048 | tf_op jit(solution)/shard_map/ppermute | solution.py:18
  44.7 19.3 %copy-start.7 = (f32[4]{0:T(128)S(1)}, f32[4]{0:T(128)}, u32[]{:S(2)}) copy-start(f32[4]{0:T(128)} %param.18) | copy-start | bytes 52
  44.7 19.2 %copy-start.8 = (f32[3]{0:T(128)S(1)}, f32[3]{0:T(128)}, u32[]{:S(2)}) copy-start(f32[3]{0:T(128)} %param.21) | copy-start | bytes 40
  72.1 237.1 %copy-start.9 = (s32[4]{0:T(128)S(1)}, s32[4]{0:T(128)}, u32[]{:S(2)}) copy-start(s32[4]{0:T(128)} %param.15) | copy-start | bytes 52
  78.9 323.4 %all-to-all-start = ((f32[1,4,128,2048]{3,1,0,2:T(4,128)}), f32[1,4,128,2048]{3,1,0,2:T(4,128)}, u32[]{:S(2)}, u32[]{:S(2)}) async-start(f32[1,4,128,2048]{3,1,0,2:T(4,128)} %bitcast.118), calls=%async_computation | async-start | bytes 8388608 | tf_op jit(solution)/shard_map/all_to_all | solution.py:102
  429.4 1.0 copy-start.3
where the time goes:
time: 438 us; the launch traced here: 431 us
  starting transfers between devices  239 us (55%)
  waiting for transfers between devices  95 us (22%)
  local copies, waits for them, and re-layouts  71 us (16%)
  other arithmetic  18.4 us (4%)
  loops' own time  5.73 us (1%)
    all_to_all x1, starting transfers between devices, per_device(): lax.all_to_all(layer_image[None], 'depth', split_axis=2, concat_axis=0, t...  230 us
    all_to_all x1, waiting for transfers between devices, per_device(): lax.all_to_all(layer_image[None], 'depth', split_axis=2, concat_axis=0, t...  93.1 us
    concatenate x2, local copies, waits for them, and re-layouts, with_halo(): x = jnp.concatenate([before, x, after], axis=dim)  30.2 us
    unnamed x11, local copies, waits for them, and re-layouts  17.3 us
  transfers between devices with their start and end apart: 5, of which 2 were waited for; matrix products, arithmetic and copies ran while one was open for 3% of the time, Pallas kernels for 0%

commit v1 on v0

v1 whole, which is shorter than its diff:
```python
import math

import jax
import jax.numpy as jnp
from jax import lax
from jax.experimental import pallas as pl
from jax.experimental.pallas import tpu as pltpu
from jax.sharding import PartitionSpec as P

absorption = 0.08
LANES = 128
SUB = 8
LOG_MID = -12.5
LOG_HALF = 16.0
LOG_STEPS = 32767
LOW = -LOG_STEPS
VALUE_FLOOR = 2.0 ** (LOG_MID - LOG_HALF)


def encode(value):
    scale = LOG_STEPS / LOG_HALF
    log2v = jnp.log(jnp.maximum(value, VALUE_FLOOR)) * (scale / math.log(2.0))
    shifted = jnp.clip(log2v + (32768.5 - LOG_MID * scale), 1.0, 65535.5)
    return (shifted.astype(jnp.int32) - 32768).astype(jnp.int16)


def decode(code):
    wide = code.astype(jnp.int32).astype(jnp.float32)
    value = jnp.exp2(wide * (LOG_HALF / LOG_STEPS) + LOG_MID)
    return jnp.where(wide > LOW, value, 0.0)


def table(bump_center, bump_width, bump_height, bump_color, light_dir, depth_len):
    log2e = math.log2(math.e)
    strength = bump_height * (absorption / depth_len * log2e)
    square = -log2e / (2.0 * bump_width * bump_width)
    linear = -2.0 * square * bump_center
    constant = square * bump_center * bump_center + jnp.log2(strength)
    color = bump_color / strength[None]
    return jnp.concatenate([square, linear, constant, 0.7 * light_dir, color.reshape(-1)])


def march(volume, coef, info, row_halo, left_halo, right_halo, start, count, tiles, bumps, parts):
    planes, rows, cols = volume.shape
    depth_len = planes - 2
    width = tiles * LANES
    steps = count // tiles
    all_tiles = cols // LANES
    block = rows // parts
    has_left = left_halo is not None
    has_right = right_halo is not None

    def body(info_ref, coef_ref, vol, left, right, halo, *rest):
        rest = list(rest)
        lh = rest.pop(0) if has_left else None
        rh = rest.pop(0) if has_right else None
        outs, (cells, layer) = rest[:parts], rest[parts:]
        step = pl.program_id(0)
        me, row_at, row_last, is_empty = info_ref[0], info_ref[1], info_ref[2], info_ref[3]

        @pl.when(is_empty == 1)
        def _():
            outs[0][...] = jnp.zeros(outs[0].shape, jnp.float32)
            for k in range(1, parts):
                outs[k][...] = jnp.full(outs[k].shape, LOW, jnp.int16)

        @pl.when(is_empty != 1)
        def _():
            top_on = (row_at > 0).astype(jnp.float32)
            bottom_on = (row_at < row_last).astype(jnp.float32)
            for t in range(tiles):
                span = slice(LANES * t, LANES * (t + 1))
                cells[t + 1, :, SUB : SUB + rows, :] = vol[:, :, span].astype(jnp.float32)
                edge = halo[:, :, span].astype(jnp.float32)
                cells[t + 1, :, 0:SUB, :] = jnp.broadcast_to(edge[:, :1] * top_on, (planes, SUB, LANES))
                cells[t + 1, :, SUB + rows :, :] = jnp.broadcast_to(
                    edge[:, -1:] * bottom_on, (planes, SUB, LANES)
                )
            cells[0, :, SUB : SUB + rows, :] = left[...].astype(jnp.float32)
            cells[tiles + 1, :, SUB : SUB + rows, :] = right[...].astype(jnp.float32)
            if has_left:
                @pl.when(step == 0)
                def _():
                    cells[0, :, SUB : SUB + rows, :] = lh[...].astype(jnp.float32)
            if has_right:
                @pl.when(step == steps - 1)
                def _():
                    cells[tiles + 1, :, SUB : SUB + rows, :] = rh[...].astype(jnp.float32)

            square = [coef_ref[k] for k in range(bumps)]
            linear = [coef_ref[bumps + k] for k in range(bumps)]
            constant = [coef_ref[2 * bumps + k] for k in range(bumps)]
            light = [coef_ref[3 * bumps + k] for k in range(3)]
            color = [[coef_ref[3 * bumps + 3 + bumps * c + k] for k in range(bumps)] for c in range(3)]
            lane = lax.broadcasted_iota(jnp.int32, (SUB, LANES), 1)
            first = lane == 0
            last = lane == LANES - 1

            def strip(i, carry):
                base = pl.multiple_of(i * SUB, SUB)

                def load(t, s, shift=0):
                    return cells[t, s, pl.ds(base + (SUB + shift), SUB), :]

                zero = jnp.zeros((SUB, LANES), jnp.float32)
                before = [load(t + 1, 0) for t in range(tiles)]
                here = [load(t + 1, 1) for t in range(tiles)]
                depth = [zero] * tiles
                through = [zero + 1.0] * tiles
                total = [[zero] * bumps for t in range(tiles)]
                for s in range(1, depth_len + 1):
                    ahead = [load(t + 1, s + 1) for t in range(tiles)]
                    line = [load(0, s)] + here + [load(tiles + 1, s)]
                    up = [pltpu.roll(x, 1, 1) for x in line[:-1]]
                    down = [pltpu.roll(x, LANES - 1, 1) for x in line[1:]]
                    down.append(down[-1])
                    for t in range(tiles):
                        f = here[t]
                        grad_z = ahead[t] - before[t]
                        grad_y = load(t + 1, s, 1) - load(t + 1, s, -1)
                        right_of = jnp.where(last, pltpu.roll(line[t + 2], LANES - 1, 1), down[t])
                        left_of = jnp.where(first, up[t], pltpu.roll(line[t + 1], 1, 1))
                        grad_x = right_of - left_of
                        facing = jnp.abs(light[0] * grad_z + light[1] * grad_y + light[2] * grad_x)
                        norm = grad_z * grad_z + grad_y * grad_y + grad_x * grad_x + 4.0
                        shading = 0.3 + facing * lax.rsqrt(norm)
                        bump = [
                            jnp.exp2((square[k] * f + linear[k]) * f + constant[k]) for k in range(bumps)
                        ]
                        for k in range(bumps):
                            depth[t] = depth[t] - bump[k]
                        passed = jnp.exp2(depth[t])
                        weight = (through[t] - passed) * shading
                        through[t] = passed
                        total[t] = [total[t][k] + weight * bump[k] for k in range(bumps)]
                    before, here = here, ahead
                for t in range(tiles):
                    for c in range(3):
                        mixed = color[c][0] * total[t][0]
                        for k in range(1, bumps):
                            mixed = mixed + color[c][k] * total[t][k]
                        layer[c, pl.ds(base, SUB), LANES * t : LANES * (t + 1)] = mixed
                    layer[3, pl.ds(base, SUB), LANES * t : LANES * (t + 1)] = 1.0 - through[t]
                return carry

            lax.fori_loop(0, rows // SUB, strip, 0)
            for k in range(parts):
                at = pl.multiple_of(lax.rem(me + k, parts) * block, block)
                value = layer[:, pl.ds(at, block), :]
                outs[k][...] = value if k == 0 else encode(value)

    chunk = count * LANES
    tile0 = start // tiles
    in_specs = [
        pl.BlockSpec(memory_space=pltpu.SMEM),
        pl.BlockSpec(memory_space=pltpu.SMEM),
        pl.BlockSpec((planes, rows, width), lambda i: (0, 0, tile0 + i)),
        pl.BlockSpec((planes, rows, LANES), lambda i: (0, 0, jnp.maximum(start + i * tiles - 1, 0))),
        pl.BlockSpec(
            (planes, rows, LANES), lambda i: (0, 0, jnp.minimum(start + (i + 1) * tiles, all_tiles - 1))
        ),
        pl.BlockSpec((planes, row_halo.shape[1], width), lambda i: (0, 0, tile0 + i)),
    ]
    operands = [info, coef, volume, volume, volume, row_halo]
    for halo in (left_halo, right_halo):
        if halo is not None:
            in_specs.append(pl.BlockSpec((planes, rows, LANES), lambda i: (0, 0, 0)))
            operands.append(halo)
    return pl.pallas_call(
        body,
        grid=(steps,),
        out_shape=[
            jax.ShapeDtypeStruct((4, block, chunk), jnp.float32 if k == 0 else jnp.int16)
            for k in range(parts)
        ],
        in_specs=in_specs,
        out_specs=[pl.BlockSpec((4, block, width), lambda i: (0, 0, i)) for k in range(parts)],
        scratch_shapes=[
            pltpu.VMEM((tiles + 2, planes, rows + 2 * SUB, LANES), jnp.float32),
            pltpu.VMEM((4, rows, width), jnp.float32),
        ],
        compiler_params=pltpu.CompilerParams(vmem_limit_bytes=48 << 20),
        name="march",
    )(*operands)


def composite(own, coded, info, order, image, start, cols):
    parts = 1 + len(coded)
    channels, block, chunk = own.shape

    def body(info_ref, order_ref, own_ref, *rest):
        codes = rest[: parts - 1]
        out, layers = rest[-2], rest[-1]
        me = info_ref[0]
        layers[0] = own_ref[...]
        for k in range(1, parts):
            layers[k] = decode(codes[k - 1][...])
        through = jnp.ones((block, chunk), jnp.float32)
        summed = [jnp.zeros((block, chunk), jnp.float32)] * channels
        for place in range(parts):
            at = lax.rem(me - order_ref[place] + parts, parts)
            summed = [summed[c] + through * layers[at, c] for c in range(channels)]
            through = through * (1.0 - layers[at, 3])
        for c in range(channels):
            out[c] = summed[c]

    smem = pl.BlockSpec(memory_space=pltpu.SMEM)
    whole = pl.BlockSpec((channels, block, chunk), lambda i: (0, 0, 0))
    at_chunk = pl.BlockSpec((channels, block, chunk), lambda i: (0, 0, start * LANES // chunk))
    in_specs = [smem, smem, whole] + [whole] * (parts - 1)
    operands = [info, order, own, *coded]
    aliases = {}
    if image is not None:
        aliases = {len(operands): 0}
        operands.append(image)
        in_specs.append(pl.BlockSpec(memory_space=pl.ANY))
    return pl.pallas_call(
        body,
        grid=(1,),
        out_shape=jax.ShapeDtypeStruct((channels, block, cols), jnp.float32),
        in_specs=in_specs,
        out_specs=at_chunk,
        scratch_shapes=[pltpu.VMEM((parts, channels, block, chunk), jnp.float32)],
        input_output_aliases=aliases,
        compiler_params=pltpu.CompilerParams(vmem_limit_bytes=48 << 20),
        name="composite",
    )(*operands)


def per_device(volume, order, empty, bump_center, bump_width, bump_height, bump_color, light_dir):
    volume = volume[0]
    planes, rows, cols = volume.shape
    parts = lax.axis_size("depth")
    n_row = lax.axis_size("row")
    n_col = lax.axis_size("col")
    bumps = bump_center.shape[0]
    row_at = lax.axis_index("row")

    up = [(i, i + 1) for i in range(n_row - 1)]
    down = [(i + 1, i) for i in range(n_row - 1)]
    if n_row == 2:
        edge = lax.dynamic_slice(volume, (0, jnp.where(row_at == 0, rows - 1, 0), 0), (planes, 1, cols))
        row_halo = lax.ppermute(edge, "row", up + down)
    else:
        row_halo = jnp.concatenate(
            [
                lax.ppermute(volume[:, -1:], "row", up),
                lax.ppermute(volume[:, :1], "row", down),
            ],
            axis=1,
        )
    left_halo = lax.ppermute(volume[:, :, -LANES:], "col", [(i, i + 1) for i in range(n_col - 1)])
    right_halo = lax.ppermute(volume[:, :, :LANES], "col", [(i + 1, i) for i in range(n_col - 1)])

    coef = table(bump_center, bump_width, bump_height, bump_color, light_dir, planes - 2)
    me = lax.axis_index("depth")
    info = jnp.stack([me, row_at, jnp.int32(n_row - 1), empty[0, 0, 0]]).astype(jnp.int32)

    all_tiles = cols // LANES
    chunks = 4
    count = all_tiles // chunks
    image = None
    waiting = []
    for at in [1, 2, 0, 3]:
        start = at * count
        blocks = march(
            volume,
            coef,
            info,
            row_halo,
            left_halo if at == 0 else None,
            right_halo if at == chunks - 1 else None,
            start,
            count,
            2,
            bumps,
            parts,
        )
        coded = [
            lax.ppermute(blocks[k], "depth", [(i, (i + k) % parts) for i in range(parts)])
            for k in range(1, parts)
        ]
        waiting.append((start, blocks[0], coded))
    for start, own, coded in waiting:
        image = composite(own, coded, info, order, image, start, cols)
    return image[None]


def solution(mesh):
    placed = (
        P("depth", None, "row", "col"),
        P(),
        P("depth", "row", "col"),
        P(),
        P(),
        P(),
        P(),
        P(),
    )
    return jax.shard_map(
        per_device,
        mesh=mesh,
        in_specs=placed,
        out_specs=P("row", None, "depth", "col"),
        check_vma=False,
    )
```

time: 438 us -> 90 us (0.21)
  the two profiles are of different devices: /device:TPU:0 before, /device:TPU:29 now
where the time goes in v1:
time: 90 us; the launch traced here: 88.5 us
  Pallas kernels  51.1 us (57%)
  starting transfers between devices  17.9 us (20%)
  waiting for transfers between devices  13.1 us (15%)
  other arithmetic  2.79 us (3%)
  local copies, waits for them, and re-layouts  2.76 us (3%)
    pallas_call x4, Pallas kernels, march(): pl.pallas_call(body, grid=(steps,), out_shape=[jax.ShapeDtypeStruct((4, b...  44.8 us
    ppermute x12, waiting for transfers between devices, per_device(): lax.ppermute(blocks[k], 'depth', [(i, (i + k) % parts) for i in range(par...  13.1 us
    ppermute x12, starting transfers between devices, per_device(): lax.ppermute(blocks[k], 'depth', [(i, (i + k) % parts) for i in range(par...  11 us
    pallas_call x4, Pallas kernels, composite(): pl.pallas_call(body, grid=(1,), out_shape=jax.ShapeDtypeStruct((channels,...  6.27 us
    ppermute x1, starting transfers between devices, per_device(): lax.ppermute(volume[:, :, -LANES:], 'col', [(i, i + 1) for i in range(n_c...  3.12 us
    ppermute x1, starting transfers between devices, per_device(): lax.ppermute(volume[:, :, :LANES], 'col', [(i + 1, i) for i in range(n_co...  3.06 us
  transfers between devices with their start and end apart: 15, of which 2 were waited for; matrix products, arithmetic and copies ran while one was open for 5% of the time, Pallas kernels for 56%

profile of v1, /device:TPU:29, one launch (start us, length us, event | category | flops | bytes accessed | tf_op | source)
XLA Modules:
  0.0 88.5 jit_solution(7552062575886365805)
XLA Ops:
  0.0 1.2 %dynamic-slice_bitcast_fusion = bf16[18,1,2048]{2,1,0:T(2,128)(2,1)S(1)} fusion(bf16[1,18,128,2048]{3,2,1,0:T(8,128)(2,1)} %param.8, s32[]{:T(128)S(6)} %select_n.5), kind=kLoop, calls=%fused_computation | loop fusion | bytes 147460 | tf_op jit(solution)/shard_map/dynamic_slice | solution.py:242
  1.2 0.7 collective-permute-start
  2.0 1.4 %fusion.3 = (bf16[18,128,128]{2,1,0:T(8,128)(2,1)S(1)}, bf16[18,128,128]{2,1,0:T(8,128)(2,1)S(1)}) fusion(bf16[18,128,2048]{2,1,0:T(8,128)(2,1)} %bitcast.8), kind=kLoop, calls=%fused_computation.10 | loop fusion | bytes 2359296 | tf_op jit(solution)/shard_map/slice | solution.py:252
  3.3 3.1 %collective-permute-start.5 = (bf16[18,128,128]{2,1,0:T(8,128)(2,1)S(1)}, bf16[18,128,128]{2,1,0:T(8,128)(2,1)S(1)}, u32[]{:S(2)}, u32[]{:S(2)}) collective-permute-start(bf16[18,128,128]{2,1,0:T(8,128)(2,1)S(1)} %get-tuple-element.39), channel_id=1, source_target_pairs={{0,1},{1,2},{2,3},{4,5},{5,6},{6,7},{8,9},{9,10},{10,11},{12,13},{... | collective-permute-start | bytes 1769480 | tf_op jit(solution)/shard_map/ppermute | solution.py:252
  6.5 3.1 %collective-permute-start.1 = (bf16[18,128,128]{2,1,0:T(8,128)(2,1)S(1)}, bf16[18,128,128]{2,1,0:T(8,128)(2,1)S(1)}, u32[]{:S(2)}, u32[]{:S(2)}) collective-permute-start(bf16[18,128,128]{2,1,0:T(8,128)(2,1)S(1)} %get-tuple-element.40), channel_id=1, source_target_pairs={{1,0},{2,1},{3,2},{5,4},{6,5},{7,6},{9,8},{10,9},{11,10},{13,12},{... | collective-permute-start | bytes 1769480 | tf_op jit(solution)/shard_map/ppermute | solution.py:253
  10.2 0.7 fusion.1
  10.9 0.7 broadcast_divide_fusion
  11.6 0.1 reshape.5
  11.7 0.7 broadcast_multiply_fusion
  12.3 0.7 multiply_multiply_fusion.2
  13.0 0.1 concatenate.3.coef_ref
  13.1 0.1 pad_add_fusion.info_ref
  13.2 11.2 %march.7 = (f32[4,32,512]{2,1,0:T(8,128)S(1)}, s16[4,32,512]{2,1,0:T(8,128)(2,1)S(1)}, s16[4,32,512]{2,1,0:T(8,128)(2,1)S(1)}, s16[4,32,512]{2,1,0:T(8,128)(2,1)S(1)}) custom-call(s32[4]{0:T(128)S(1)} %pad_add_fusion.info_ref, f32[27]{0:T(128)S(1)} %concatenate.3.coef_ref, bf16[18,128,2048]{2,1,0:T(8,128)(2,1)} %bitcast.9, bf16[18,128,2048]{2,1,0:T(8,128)(2,1)} %bitcast.10, ...), custom_call_target="tpu_custom_call" | custom-call | tf_op jit(solution)/shard_map/march/pallas_call | solution.py:169
  24.4 0.1 collective-permute-start.13
  24.5 1.4 %collective-permute-start.14 = (s16[4,32,512]{2,1,0:T(8,128)(2,1)S(1)}, s16[4,32,512]{2,1,0:T(8,128)(2,1)S(1)}, u32[]{:S(2)}, u32[]{:S(2)}) collective-permute-start(s16[4,32,512]{2,1,0:T(8,128)(2,1)S(1)} %get-tuple-element.36), channel_id=1, source_target_pairs={{0,24},{8,0},{16,8},{24,16},{1,25},{9,1},{17,9},{25,17},{2,26},{10... | collective-permute-start | bytes 393224 | tf_op jit(solution)/shard_map/ppermute | solution.py:280
  25.8 11.1 %march.6 = (f32[4,32,512]{2,1,0:T(8,128)S(1)}, s16[4,32,512]{2,1,0:T(8,128)(2,1)S(1)}, s16[4,32,512]{2,1,0:T(8,128)(2,1)S(1)}, s16[4,32,512]{2,1,0:T(8,128)(2,1)S(1)}) custom-call(s32[4]{0:T(128)S(1)} %pad_add_fusion.info_ref, f32[27]{0:T(128)S(1)} %concatenate.3.coef_ref, bf16[18,128,2048]{2,1,0:T(8,128)(2,1)} %bitcast.12, bf16[18,128,2048]{2,1,0:T(8,128)(2,1)} %bitcast.13, ...), custom_call_target="tpu_custom_call" | custom-call | tf_op jit(solution)/shard_map/march/pallas_call | solution.py:169
  37.0 2.1 %collective-permute-start.9 = (s16[4,32,512]{2,1,0:T(8,128)(2,1)S(1)}, s16[4,32,512]{2,1,0:T(8,128)(2,1)S(1)}, u32[]{:S(2)}, u32[]{:S(2)}) collective-permute-start(s16[4,32,512]{2,1,0:T(8,128)(2,1)S(1)} %get-tuple-element.30), channel_id=1, source_target_pairs={{0,8},{8,16},{16,24},{24,0},{1,9},{9,17},{17,25},{25,1},{2,10},{10... | collective-permute-start | bytes 393224 | tf_op jit(solution)/shard_map/ppermute | solution.py:280
  39.1 11.3 %march.5 = (f32[4,32,512]{2,1,0:T(8,128)S(1)}, s16[4,32,512]{2,1,0:T(8,128)(2,1)S(1)}, s16[4,32,512]{2,1,0:T(8,128)(2,1)S(1)}, s16[4,32,512]{2,1,0:T(8,128)(2,1)S(1)}) custom-call(s32[4]{0:T(128)S(1)} %pad_add_fusion.info_ref, f32[27]{0:T(128)S(1)} %concatenate.3.coef_ref, bf16[18,128,2048]{2,1,0:T(8,128)(2,1)} %bitcast.15, bf16[18,128,2048]{2,1,0:T(8,128)(2,1)} %bitcast.16, ...), custom_call_target="tpu_custom_call" | custom-call | tf_op jit(solution)/shard_map/march/pallas_call | solution.py:169
  50.4 0.1 collective-permute-start.10
  50.5 0.3 collective-permute-start.11
  50.8 3.0 %collective-permute-start.6 = (s16[4,32,512]{2,1,0:T(8,128)(2,1)S(1)}, s16[4,32,512]{2,1,0:T(8,128)(2,1)S(1)}, u32[]{:S(2)}, u32[]{:S(2)}) collective-permute-start(s16[4,32,512]{2,1,0:T(8,128)(2,1)S(1)} %get-tuple-element.26), channel_id=1, source_target_pairs={{0,8},{8,16},{16,24},{24,0},{1,9},{9,17},{17,25},{25,1},{2,10},{10... | collective-permute-start | bytes 393224 | tf_op jit(solution)/shard_map/ppermute | solution.py:280
  53.8 11.3 %march.4 = (f32[4,32,512]{2,1,0:T(8,128)S(1)}, s16[4,32,512]{2,1,0:T(8,128)(2,1)S(1)}, s16[4,32,512]{2,1,0:T(8,128)(2,1)S(1)}, s16[4,32,512]{2,1,0:T(8,128)(2,1)S(1)}) custom-call(s32[4]{0:T(128)S(1)} %pad_add_fusion.info_ref, f32[27]{0:T(128)S(1)} %concatenate.3.coef_ref, bf16[18,128,2048]{2,1,0:T(8,128)(2,1)} %bitcast.18, bf16[18,128,2048]{2,1,0:T(8,128)(2,1)} %bitcast.19, ...), custom_call_target="tpu_custom_call" | custom-call | tf_op jit(solution)/shard_map/march/pallas_call | solution.py:169
  65.1 0.1 collective-permute-start.7
  65.2 0.5 collective-permute-start.8
  65.8 2.8 %collective-permute-start.2 = (s16[4,32,512]{2,1,0:T(8,128)(2,1)S(1)}, s16[4,32,512]{2,1,0:T(8,128)(2,1)S(1)}, u32[]{:S(2)}, u32[]{:S(2)}) collective-permute-start(s16[4,32,512]{2,1,0:T(8,128)(2,1)S(1)} %get-tuple-element.22), channel_id=1, source_target_pairs={{0,8},{8,16},{16,24},{24,0},{1,9},{9,17},{17,25},{25,1},{2,10},{10... | collective-permute-start | bytes 393224 | tf_op jit(solution)/shard_map/ppermute | solution.py:280
  68.5 0.5 collective-permute-start.3
  69.1 1.6 %composite.4.rest_3_ = f32[4,32,2048]{2,1,0:T(8,128)} custom-call(s32[4]{0:T(128)S(1)} %pad_add_fusion.info_ref, s32[4]{0:T(128)S(1)} %copy-done, f32[4,32,512]{2,1,0:T(8,128)S(1)} %get-tuple-element.33.own_ref, s16[4,32,512]{2,1,0:T(8,128)(2,1)S(1)} %collective-permute-done.12.rest_0_, s16[4,32,512]{2,1,0:T(8,128)(2,1)S(1)} %collective-permute-done.13.rest_1_, ...), custom_call_target="tpu_custom_call" | custom-call | tf_op jit(solution)/shard_map/composite/pallas_call | solution.py:217
  70.7 1.6 %composite.5.rest_3_ = f32[4,32,2048]{2,1,0:T(8,128)} custom-call(s32[4]{0:T(128)S(1)} %pad_add_fusion.info_ref, s32[4]{0:T(128)S(1)} %copy-done, f32[4,32,512]{2,1,0:T(8,128)S(1)} %get-tuple-element.29.own_ref, s16[4,32,512]{2,1,0:T(8,128)(2,1)S(1)} %collective-permute-done.9.rest_0_, ...), custom_call_target="tpu_custom_call", output_to_operand_aliasing={{}: (6, {})} | custom-call | tf_op jit(solution)/shard_map/composite/pallas_call | solution.py:217
  72.2 5.0 %collective-permute-done.7.rest_1_ = s16[4,32,512]{2,1,0:T(8,128)(2,1)S(1)} collective-permute-done((s16[4,32,512]{2,1,0:T(8,128)(2,1)S(1)}, s16[4,32,512]{2,1,0:T(8,128)(2,1)S(1)}, u32[]{:S(2)}, u32[]{:S(2)}) %collective-permute-start.7) | collective-permute-done | bytes 131104 | tf_op jit(solution)/shard_map/ppermute | solution.py:280
  77.3 1.6 %composite.6.rest_3_ = f32[4,32,2048]{2,1,0:T(8,128)} custom-call(s32[4]{0:T(128)S(1)} %pad_add_fusion.info_ref, s32[4]{0:T(128)S(1)} %copy-done, f32[4,32,512]{2,1,0:T(8,128)S(1)} %get-tuple-element.25.own_ref, s16[4,32,512]{2,1,0:T(8,128)(2,1)S(1)} %collective-permute-done.6.rest_0_, ...), custom_call_target="tpu_custom_call", output_to_operand_aliasing={{}: (6, {})} | custom-call | tf_op jit(solution)/shard_map/composite/pallas_call | solution.py:217
  78.8 8.0 %collective-permute-done.3.rest_1_ = s16[4,32,512]{2,1,0:T(8,128)(2,1)S(1)} collective-permute-done((s16[4,32,512]{2,1,0:T(8,128)(2,1)S(1)}, s16[4,32,512]{2,1,0:T(8,128)(2,1)S(1)}, u32[]{:S(2)}, u32[]{:S(2)}) %collective-permute-start.3) | collective-permute-done | bytes 131104 | tf_op jit(solution)/shard_map/ppermute | solution.py:280
  86.9 1.6 %composite.7 = f32[4,32,2048]{2,1,0:T(8,128)} custom-call(s32[4]{0:T(128)S(1)} %pad_add_fusion.info_ref, s32[4]{0:T(128)S(1)} %copy-done, f32[4,32,512]{2,1,0:T(8,128)S(1)} %get-tuple-element.21.own_ref, s16[4,32,512]{2,1,0:T(8,128)(2,1)S(1)} %collective-permute-done.2.rest_0_, ...), custom_call_target="tpu_custom_call", output_to_operand_aliasing={{}: (6, {})} | custom-call | tf_op jit(solution)/shard_map/composite/pallas_call | solution.py:217
  (17 shorter events, 0.2 us)
Async XLA Ops:
  1.2 11.9 %collective-permute-start = (bf16[18,1,2048]{2,1,0:T(2,128)(2,1)S(1)}, bf16[18,1,2048]{2,1,0:T(2,128)(2,1)S(1)}, u32[]{:S(2)}, u32[]{:S(2)}) collective-permute-start(bf16[18,1,2048]{2,1,0:T(2,128)(2,1)S(1)} %dynamic-slice_bitcast_fusion), channel_id=1, source_target_pairs={{0,4},{4,0},{1,5},{5,1},{2,6},{6,2},{3,7},{7,3},{8,12},{12,8},{9,1... | collective-permute-start | bytes 221192 | tf_op jit(solution)/shard_map/ppermute | solution.py:243
  3.3 33.6 %collective-permute-start.5 = (bf16[18,128,128]{2,1,0:T(8,128)(2,1)S(1)}, bf16[18,128,128]{2,1,0:T(8,128)(2,1)S(1)}, u32[]{:S(2)}, u32[]{:S(2)}) collective-permute-start(bf16[18,128,128]{2,1,0:T(8,128)(2,1)S(1)} %get-tuple-element.39), channel_id=1, source_target_pairs={{0,1},{1,2},{2,3},{4,5},{5,6},{6,7},{8,9},{9,10},{10,11},{12,13},{... | collective-permute-start | bytes 1769480 | tf_op jit(solution)/shard_map/ppermute | solution.py:252
  6.5 44.4 %collective-permute-start.1 = (bf16[18,128,128]{2,1,0:T(8,128)(2,1)S(1)}, bf16[18,128,128]{2,1,0:T(8,128)(2,1)S(1)}, u32[]{:S(2)}, u32[]{:S(2)}) collective-permute-start(bf16[18,128,128]{2,1,0:T(8,128)(2,1)S(1)} %get-tuple-element.40), channel_id=1, source_target_pairs={{1,0},{2,1},{3,2},{5,4},{6,5},{7,6},{9,8},{10,9},{11,10},{13,12},{... | collective-permute-start | bytes 1769480 | tf_op jit(solution)/shard_map/ppermute | solution.py:253
  24.3 26.1 %collective-permute-start.12 = (s16[4,32,512]{2,1,0:T(8,128)(2,1)S(1)}, s16[4,32,512]{2,1,0:T(8,128)(2,1)S(1)}, u32[]{:S(2)}, u32[]{:S(2)}) collective-permute-start(s16[4,32,512]{2,1,0:T(8,128)(2,1)S(1)} %get-tuple-element.34), channel_id=1, source_target_pairs={{0,8},{8,16},{16,24},{24,0},{1,9},{9,17},{17,25},{25,1},{2,10},{10... | collective-permute-start | bytes 393224 | tf_op jit(solution)/shard_map/ppermute | solution.py:280
  24.4 26.1 %collective-permute-start.13 = (s16[4,32,512]{2,1,0:T(8,128)(2,1)S(1)}, s16[4,32,512]{2,1,0:T(8,128)(2,1)S(1)}, u32[]{:S(2)}, u32[]{:S(2)}) collective-permute-start(s16[4,32,512]{2,1,0:T(8,128)(2,1)S(1)} %get-tuple-element.35), channel_id=1, source_target_pairs={{0,16},{8,24},{16,0},{24,8},{1,17},{9,25},{17,1},{25,9},{2,18},{10... | collective-permute-start | bytes 393224 | tf_op jit(solution)/shard_map/ppermute | solution.py:280
  24.5 40.7 %collective-permute-start.14 = (s16[4,32,512]{2,1,0:T(8,128)(2,1)S(1)}, s16[4,32,512]{2,1,0:T(8,128)(2,1)S(1)}, u32[]{:S(2)}, u32[]{:S(2)}) collective-permute-start(s16[4,32,512]{2,1,0:T(8,128)(2,1)S(1)} %get-tuple-element.36), channel_id=1, source_target_pairs={{0,24},{8,0},{16,8},{24,16},{1,25},{9,1},{17,9},{25,17},{2,26},{10... | collective-permute-start | bytes 393224 | tf_op jit(solution)/shard_map/ppermute | solution.py:280
  37.0 28.2 %collective-permute-start.9 = (s16[4,32,512]{2,1,0:T(8,128)(2,1)S(1)}, s16[4,32,512]{2,1,0:T(8,128)(2,1)S(1)}, u32[]{:S(2)}, u32[]{:S(2)}) collective-permute-start(s16[4,32,512]{2,1,0:T(8,128)(2,1)S(1)} %get-tuple-element.30), channel_id=1, source_target_pairs={{0,8},{8,16},{16,24},{24,0},{1,9},{9,17},{17,25},{25,1},{2,10},{10... | collective-permute-start | bytes 393224 | tf_op jit(solution)/shard_map/ppermute | solution.py:280
  50.4 15.3 %collective-permute-start.10 = (s16[4,32,512]{2,1,0:T(8,128)(2,1)S(1)}, s16[4,32,512]{2,1,0:T(8,128)(2,1)S(1)}, u32[]{:S(2)}, u32[]{:S(2)}) collective-permute-start(s16[4,32,512]{2,1,0:T(8,128)(2,1)S(1)} %get-tuple-element.31), channel_id=1, source_target_pairs={{0,16},{8,24},{16,0},{24,8},{1,17},{9,25},{17,1},{25,9},{2,18},{10... | collective-permute-start | bytes 393224 | tf_op jit(solution)/shard_map/ppermute | solution.py:280
  50.5 18.0 %collective-permute-start.11 = (s16[4,32,512]{2,1,0:T(8,128)(2,1)S(1)}, s16[4,32,512]{2,1,0:T(8,128)(2,1)S(1)}, u32[]{:S(2)}, u32[]{:S(2)}) collective-permute-start(s16[4,32,512]{2,1,0:T(8,128)(2,1)S(1)} %get-tuple-element.32), channel_id=1, source_target_pairs={{0,24},{8,0},{16,8},{24,16},{1,25},{9,1},{17,9},{25,17},{2,26},{10... | collective-permute-start | bytes 393224 | tf_op jit(solution)/shard_map/ppermute | solution.py:280
  50.8 18.3 %copy-start = (s32[4]{0:T(128)S(1)}, s32[4]{0:T(128)}, u32[]{:S(2)}) copy-start(s32[4]{0:T(128)} %order_ref.7) | copy-start | bytes 52
  50.8 18.2 %collective-permute-start.6 = (s16[4,32,512]{2,1,0:T(8,128)(2,1)S(1)}, s16[4,32,512]{2,1,0:T(8,128)(2,1)S(1)}, u32[]{:S(2)}, u32[]{:S(2)}) collective-permute-start(s16[4,32,512]{2,1,0:T(8,128)(2,1)S(1)} %get-tuple-element.26), channel_id=1, source_target_pairs={{0,8},{8,16},{16,24},{24,0},{1,9},{9,17},{17,25},{25,1},{2,10},{10... | collective-permute-start | bytes 393224 | tf_op jit(solution)/shard_map/ppermute | solution.py:280
  65.1 12.1 %collective-permute-start.7 = (s16[4,32,512]{2,1,0:T(8,128)(2,1)S(1)}, s16[4,32,512]{2,1,0:T(8,128)(2,1)S(1)}, u32[]{:S(2)}, u32[]{:S(2)}) collective-permute-start(s16[4,32,512]{2,1,0:T(8,128)(2,1)S(1)} %get-tuple-element.27), channel_id=1, source_target_pairs={{0,16},{8,24},{16,0},{24,8},{1,17},{9,25},{17,1},{25,9},{2,18},{10... | collective-permute-start | bytes 393224 | tf_op jit(solution)/shard_map/ppermute | solution.py:280
  65.2 12.0 %collective-permute-start.8 = (s16[4,32,512]{2,1,0:T(8,128)(2,1)S(1)}, s16[4,32,512]{2,1,0:T(8,128)(2,1)S(1)}, u32[]{:S(2)}, u32[]{:S(2)}) collective-permute-start(s16[4,32,512]{2,1,0:T(8,128)(2,1)S(1)} %get-tuple-element.28), channel_id=1, source_target_pairs={{0,24},{8,0},{16,8},{24,16},{1,25},{9,1},{17,9},{25,17},{2,26},{10... | collective-permute-start | bytes 393224 | tf_op jit(solution)/shard_map/ppermute | solution.py:280
  65.8 13.1 %collective-permute-start.2 = (s16[4,32,512]{2,1,0:T(8,128)(2,1)S(1)}, s16[4,32,512]{2,1,0:T(8,128)(2,1)S(1)}, u32[]{:S(2)}, u32[]{:S(2)}) collective-permute-start(s16[4,32,512]{2,1,0:T(8,128)(2,1)S(1)} %get-tuple-element.22), channel_id=1, source_target_pairs={{0,8},{8,16},{16,24},{24,0},{1,9},{9,17},{17,25},{25,1},{2,10},{10... | collective-permute-start | bytes 393224 | tf_op jit(solution)/shard_map/ppermute | solution.py:280
  68.5 18.3 %collective-permute-start.3 = (s16[4,32,512]{2,1,0:T(8,128)(2,1)S(1)}, s16[4,32,512]{2,1,0:T(8,128)(2,1)S(1)}, u32[]{:S(2)}, u32[]{:S(2)}) collective-permute-start(s16[4,32,512]{2,1,0:T(8,128)(2,1)S(1)} %get-tuple-element.23), channel_id=1, source_target_pairs={{0,16},{8,24},{16,0},{24,8},{1,17},{9,25},{17,1},{25,9},{2,18},{10... | collective-permute-start | bytes 393224 | tf_op jit(solution)/shard_map/ppermute | solution.py:280
  69.0 17.8 %collective-permute-start.4 = (s16[4,32,512]{2,1,0:T(8,128)(2,1)S(1)}, s16[4,32,512]{2,1,0:T(8,128)(2,1)S(1)}, u32[]{:S(2)}, u32[]{:S(2)}) collective-permute-start(s16[4,32,512]{2,1,0:T(8,128)(2,1)S(1)} %get-tuple-element.24), channel_id=1, source_target_pairs={{0,24},{8,0},{16,8},{24,16},{1,25},{9,1},{17,9},{25,17},{2,26},{10... | collective-permute-start | bytes 393224 | tf_op jit(solution)/shard_map/ppermute | solution.py:280

commit v2 on v1

v2 whole, which is shorter than its diff:
```python
import math

import jax
import jax.numpy as jnp
from jax import lax
from jax.experimental import pallas as pl
from jax.experimental.pallas import tpu as pltpu
from jax.sharding import PartitionSpec as P

absorption = 0.08
LOG2E = math.log2(math.e)
LANES = 128
SUB = 8
GROUP = 2
EDGES_AFTER = False
LAG = 2
STEP = 8
WIDE = 4
UNROLL = 2
LOG_MID = -12.5
LOG_HALF = 16.0
LOG_STEPS = 32767
LOW = -LOG_STEPS
VALUE_FLOOR = 2.0 ** (LOG_MID - LOG_HALF)


def encode(value):
    scale = LOG_STEPS / LOG_HALF
    log2v = jnp.log(jnp.maximum(value, VALUE_FLOOR)) * (scale / math.log(2.0))
    shifted = jnp.clip(log2v + (32768.5 - LOG_MID * scale), 1.0, 65535.5)
    return (shifted.astype(jnp.int32) - 32768).astype(jnp.int16)


def decode(code):
    wide = code.astype(jnp.int32).astype(jnp.float32)
    value = jnp.exp2(wide * (LOG_HALF / LOG_STEPS) + LOG_MID)
    return jnp.where(wide > LOW, value, 0.0)


def march(volume, params, info, row_halo, halos, shift, tile_at, count, tiles, bumps, parts):
    planes, rows, cols = volume.shape
    depth_len = planes - 2
    width = tiles * LANES
    steps = count // tiles
    all_tiles = cols // LANES
    block = rows // parts
    bands = block // SUB
    own = shift == 0
    starts = [(tile_at + i * tiles) % all_tiles for i in range(steps)]
    left_steps = [i for i, t in enumerate(starts) if t == 0]
    right_steps = [i for i, t in enumerate(starts) if t + tiles == all_tiles]
    edges = bool(left_steps or right_steps)
    unroll = min(UNROLL, bands)

    def target(info_ref):
        return lax.rem(info_ref[0] + shift, parts)

    def tile_of(i):
        return lax.rem(tile_at + i * tiles, all_tiles)

    def body(info_ref, param_ref, vol, above, below, left, right, halo, *rest):
        rest = list(rest)
        ends = rest.pop(0) if edges else None
        out, cells, layer, coef = rest
        step = pl.program_id(0)
        row_at, row_last, is_empty = info_ref[1], info_ref[2], info_ref[3]
        to = target(info_ref)

        @pl.when(is_empty == 1)
        def _():
            out[...] = jnp.full(out.shape, 0.0 if own else LOW, out.dtype)

        @pl.when(is_empty != 1)
        def _():
            for t in range(tiles):
                span = slice(LANES * t, LANES * (t + 1))
                cells[t, :, 0:SUB, :] = above[:, :, span].astype(jnp.float32)
                cells[t, :, SUB : SUB + block, :] = vol[:, :, span].astype(jnp.float32)
                cells[t, :, SUB + block :, :] = below[:, :, span].astype(jnp.float32)

            def edge_rows(at, line, switch):
                for t in range(tiles):
                    edge = halo[:, line, LANES * t : LANES * (t + 1)].astype(jnp.float32) * switch
                    cells[t, :, at : at + SUB, :] = jnp.broadcast_to(edge, (planes, SUB, LANES))

            @pl.when(to == 0)
            def _():
                edge_rows(0, slice(0, 1), (row_at > 0).astype(jnp.float32))

            @pl.when(to == parts - 1)
            def _():
                lines = row_halo.shape[1]
                edge_rows(SUB + block, slice(lines - 1, lines), (row_at < row_last).astype(jnp.float32))

            low_half = lax.broadcasted_iota(jnp.int32, (planes, block, LANES), 2) < LANES // 2

            def side(right_tile, left_tile):
                mixed = jnp.where(low_half, right_tile[...], left_tile[...])
                cells[tiles, :, SUB : SUB + block, :] = mixed.astype(jnp.float32)

            side(right, left)
            for at in sorted(set(left_steps + right_steps)):
                pl.when(step == at)(
                    lambda at=at: side(ends if at in right_steps else right, ends if at in left_steps else left)
                )

            def splat(at):
                return jnp.full((SUB, LANES), param_ref[at], jnp.float32)

            square, linear, constant, mix = [], [], [], []
            for k in range(bumps):
                center, spread = splat(k), splat(bumps + k)
                strength = splat(2 * bumps + k) * (absorption / depth_len * LOG2E)
                sq = (-0.5 * LOG2E) / (spread * spread)
                square.append(sq)
                linear.append(-2.0 * sq * center)
                constant.append(sq * center * center + jnp.log(strength) * LOG2E)
                mix.append(1.0 / strength)
            color = [[splat(3 * bumps + c * bumps + k) * mix[k] for k in range(bumps)] for c in range(3)]
            light = [0.7 * splat(6 * bumps + k) for k in range(3)]
            kept = square + linear + constant + light + color[0] + color[1] + color[2]
            for k, value in enumerate(kept):
                coef[k] = value

            lane = lax.broadcasted_iota(jnp.int32, (SUB, LANES), 1)
            first = lane == 0
            last = lane == LANES - 1

            def strip(i, group):
                base = pl.multiple_of(i * SUB, SUB)
                at = list(range(group, min(group + GROUP, tiles)))
                wide = range(len(at))

                def load(t, s, shift=0):
                    return cells[t, s, pl.ds(base + (SUB + shift), SUB), :]

                values = iter([coef[k] for k in range(len(kept))])
                square = [next(values) for k in range(bumps)]
                linear = [next(values) for k in range(bumps)]
                constant = [next(values) for k in range(bumps)]
                light = [next(values) for k in range(3)]
                color = [[next(values) for k in range(bumps)] for c in range(3)]
                zero = jnp.zeros((SUB, LANES), jnp.float32)
                before = [load(t, 0) for t in at]
                here = [load(t, 1) for t in at]
                depth = [zero for t in at]
                through = [zero + 1.0 for t in at]
                total = [[zero] * bumps for t in at]
                for s in range(1, depth_len + 1):
                    ahead = [load(t, s + 1) for t in at]
                    outer_left = load(at[0] - 1 if at[0] > 0 else tiles, s)
                    outer_right = load(at[-1] + 1, s)
                    up = [pltpu.roll(x, 1, 1) for x in [outer_left] + here]
                    down = [pltpu.roll(x, LANES - 1, 1) for x in here + [outer_right]]
                    for j in wide:
                        f = here[j]
                        grad_z = ahead[j] - before[j]
                        grad_y = load(at[j], s, 1) - load(at[j], s, -1)
                        grad_x = jnp.where(last, down[j + 1], down[j]) - jnp.where(first, up[j], up[j + 1])
                        facing = jnp.abs(light[0] * grad_z + light[1] * grad_y + light[2] * grad_x)
                        norm = grad_z * grad_z + grad_y * grad_y + grad_x * grad_x + 4.0
                        shading = 0.3 + facing * lax.rsqrt(norm)
                        bump = [
                            jnp.exp2((square[k] * f + linear[k]) * f + constant[k]) for k in range(bumps)
                        ]
                        density = bump[0]
                        for k in range(1, bumps):
                            density = density + bump[k]
                        depth[j] = depth[j] - density
                        passed = jnp.exp2(depth[j])
                        weight = (through[j] - passed) * shading
                        through[j] = passed
                        total[j] = [total[j][k] + weight * bump[k] for k in range(bumps)]
                    before, here = here, ahead
                for j in wide:
                    span = slice(LANES * at[j], LANES * (at[j] + 1))
                    for c in range(3):
                        mixed = color[c][0] * total[j][0]
                        for k in range(1, bumps):
                            mixed = mixed + color[c][k] * total[j][k]
                        layer[c, pl.ds(base, SUB), span] = mixed
                    layer[3, pl.ds(base, SUB), span] = 1.0 - through[j]

            for group in range(0, tiles, GROUP):

                def some(i, carry, group=group):
                    for part in range(unroll):
                        strip(i * unroll + part, group)
                    return carry

                lax.fori_loop(0, bands // unroll, some, 0)
            out[...] = layer[...] if own else encode(layer[...])

    in_specs = [
        pl.BlockSpec(memory_space=pltpu.SMEM),
        pl.BlockSpec((planes, block, width), lambda i, n: (0, target(n), tile_of(i) // tiles)),
        pl.BlockSpec(
            (planes, SUB, width), lambda i, n: (0, jnp.maximum(target(n) * bands - 1, 0), tile_of(i) // tiles)
        ),
        pl.BlockSpec(
            (planes, SUB, width),
            lambda i, n: (0, jnp.minimum((target(n) + 1) * bands, rows // SUB - 1), tile_of(i) // tiles),
        ),
        pl.BlockSpec((planes, block, LANES), lambda i, n: (0, target(n), jnp.maximum(tile_of(i) - 1, 0))),
        pl.BlockSpec(
            (planes, block, LANES), lambda i, n: (0, target(n), jnp.minimum(tile_of(i) + tiles, all_tiles - 1))
        ),
        pl.BlockSpec((planes, row_halo.shape[1], width), lambda i, n: (0, 0, tile_of(i) // tiles)),
    ]
    operands = [params, volume, volume, volume, volume, volume, row_halo]
    if edges:
        in_specs += [pl.BlockSpec((planes, block, LANES), lambda i, n: (0, target(n), 0))]
        operands.append(halos)
    return pl.pallas_call(
        body,
        out_shape=jax.ShapeDtypeStruct((4, block, count * LANES), jnp.float32 if own else jnp.int16),
        grid_spec=pltpu.PrefetchScalarGridSpec(
            num_scalar_prefetch=1,
            grid=(steps,),
            in_specs=in_specs,
            out_specs=pl.BlockSpec((4, block, width), lambda i, n: (0, 0, i)),
            scratch_shapes=[
                pltpu.VMEM((tiles + 1, planes, block + 2 * SUB, LANES), jnp.float32),
                pltpu.VMEM((4, block, width), jnp.float32),
                pltpu.VMEM((6 * bumps + 3, SUB, LANES), jnp.float32),
            ],
        ),
        compiler_params=pltpu.CompilerParams(vmem_limit_bytes=48 << 20),
        name="march",
    )(info, *operands)


def composite(pieces, info, order, parts, wide):
    channels, block, cols = pieces[0][0][1].shape
    all_tiles = cols // LANES
    steps = all_tiles // wide
    flat = [(k, at, x) for k in range(parts) for at, x in pieces[k]]

    def index_map(at, x):
        held = x.shape[2] // (LANES * wide)

        def index(j, *scalars):
            return (0, 0, jnp.minimum(lax.rem(j + steps - at // wide, steps), held - 1))

        return index

    def body(info_ref, order_ref, *rest):
        out, layers = rest[-2], rest[-1]
        step = pl.program_id(0)
        for (k, at, x), ref in zip(flat, rest):
            held = x.shape[2] // (LANES * wide)

            def fill(k=k, ref=ref):
                layers[k] = ref[...] if k == 0 else decode(ref[...])

            if held == steps:
                fill()
            else:
                pl.when(lax.rem(step + steps - at // wide, steps) < held)(fill)
        me = info_ref[0]

        def band(i, carry):
            row = pl.ds(pl.multiple_of(i * SUB, SUB), SUB)
            through = jnp.ones((SUB, wide * LANES), jnp.float32)
            summed = [jnp.zeros((SUB, wide * LANES), jnp.float32)] * channels
            for place in range(parts):
                at = lax.rem(me - order_ref[place] + parts, parts)
                layer = [layers[at, c, row, :] for c in range(channels)]
                summed = [summed[c] + through * layer[c] for c in range(channels)]
                through = through * (1.0 - layer[3])
            for c in range(channels):
                out[c, row, :] = summed[c]
            return carry

        lax.fori_loop(0, block // SUB, band, 0)

    return pl.pallas_call(
        body,
        grid_spec=pltpu.PrefetchScalarGridSpec(
            num_scalar_prefetch=2,
            grid=(steps,),
            in_specs=[pl.BlockSpec((channels, block, wide * LANES), index_map(at, x)) for k, at, x in flat],
            out_specs=pl.BlockSpec((channels, block, wide * LANES), lambda j, *n: (0, 0, j)),
            scratch_shapes=[pltpu.VMEM((parts, channels, block, wide * LANES), jnp.float32)],
        ),
        out_shape=jax.ShapeDtypeStruct((channels, block, cols), jnp.float32),
        compiler_params=pltpu.CompilerParams(vmem_limit_bytes=48 << 20),
        name="composite",
    )(info, order, *[x for k, at, x in flat])


def plan(parts, all_tiles):
    half, quarter = all_tiles // 2, all_tiles // 4
    far = parts // 2
    pieces = [(k, 0, all_tiles) for k in range(1, parts) if k != far]
    pieces.insert(0, (far, quarter, half))
    pieces.insert(2, (far, quarter + half, half))
    pieces.append((0, 0, all_tiles))
    return [(k, at, count, math.gcd(STEP, quarter if k == far else count)) for k, at, count in pieces]


def per_device(volume, order, empty, bump_center, bump_width, bump_height, bump_color, light_dir):
    volume = volume[0]
    planes, rows, cols = volume.shape
    parts = lax.axis_size("depth")
    n_row = lax.axis_size("row")
    n_col = lax.axis_size("col")
    bumps = bump_center.shape[0]
    row_at = lax.axis_index("row")

    up = [(i, i + 1) for i in range(n_row - 1)]
    down = [(i + 1, i) for i in range(n_row - 1)]
    if n_row == 2:
        edge = lax.dynamic_slice(volume, (0, jnp.where(row_at == 0, rows - 1, 0), 0), (planes, 1, cols))
        row_halo = lax.ppermute(edge, "row", up + down)
    else:
        row_halo = jnp.concatenate(
            [
                lax.ppermute(volume[:, -1:], "row", up),
                lax.ppermute(volume[:, :1], "row", down),
            ],
            axis=1,
        )
    params = jnp.concatenate([bump_center, bump_width, bump_height, bump_color.reshape(-1), light_dir])
    me = lax.axis_index("depth")
    info = jnp.stack([me, row_at, jnp.int32(n_row - 1), empty[0, 0, 0]]).astype(jnp.int32)

    all_tiles = cols // LANES
    pieces = {k: [] for k in range(parts)}
    halos = None
    sent = []
    marched = []
    for turn, (shift, at, count, tiles) in enumerate(plan(parts, all_tiles)):
        if halos is None and (turn == 1 or not EDGES_AFTER):
            ends = (volume[:, :, cols - 1], volume[:, :, 0])
            if EDGES_AFTER:
                *ends, _ = lax.optimization_barrier((*ends, marched[0]))
            before = lax.ppermute(ends[0], "col", [(i, i + 1) for i in range(n_col - 1)])
            after = lax.ppermute(ends[1], "col", [(i + 1, i) for i in range(n_col - 1)])
            low_half = lax.broadcasted_iota(jnp.int32, (planes, rows, LANES), 2) < LANES // 2
            halos = jnp.where(low_half, after[:, :, None], before[:, :, None])
        if turn > 0:
            params, _ = lax.optimization_barrier((params, marched[-1]))
        if turn >= LAG:
            sent[turn - LAG], params = lax.optimization_barrier((sent[turn - LAG], params))
        layer = march(volume, params, info, row_halo, halos, shift, at, count, tiles, bumps, parts)
        marched.append(layer)
        if shift != 0:
            layer = lax.ppermute(layer, "depth", [(i, (i + shift) % parts) for i in range(parts)])
        pieces[shift].append((at, len(sent)))
        sent.append(layer)
    pieces = {k: [(at, sent[n]) for at, n in held] for k, held in pieces.items()}
    return composite(pieces, info, order, parts, math.gcd(WIDE, all_tiles // 4))[None]


def solution(mesh):
    placed = (
        P("depth", None, "row", "col"),
        P(),
        P("depth", "row", "col"),
        P(),
        P(),
        P(),
        P(),
        P(),
    )
    return jax.shard_map(
        per_device,
        mesh=mesh,
        in_specs=placed,
        out_specs=P("row", None, "depth", "col"),
        check_vma=False,
    )
```

time: 90 us -> 117 us (1.30)
  the two profiles are of different devices: /device:TPU:29 before, /device:TPU:26 now
where the time goes in v2:
time: 117 us
  Pallas kernels  52.2 us (45%)
  waiting for transfers between devices  46.3 us (40%)
  starting transfers between devices  11.7 us (10%)
  local copies, waits for them, and re-layouts  4.6 us (4%)
    pallas_call x5, Pallas kernels, march(): pl.pallas_call(body, out_shape=jax.ShapeDtypeStruct((4, block, count * LA...  49 us
    ppermute x4, waiting for transfers between devices, per_device(): lax.ppermute(layer, 'depth', [(i, (i + shift) % parts) for i in range(par...  46.3 us
    ppermute x4, starting transfers between devices, per_device(): lax.ppermute(layer, 'depth', [(i, (i + shift) % parts) for i in range(par...  4.9 us
    ppermute x1, starting transfers between devices, per_device(): lax.ppermute(ends[0], 'col', [(i, i + 1) for i in range(n_col - 1)])  4.3 us
    pallas_call x1, Pallas kernels, composite(): pl.pallas_call(body, grid_spec=pltpu.PrefetchScalarGridSpec(num_scalar_pr...  3.3 us
    ppermute x1, starting transfers between devices, per_device(): after = lax.ppermute(ends[1], 'col', [(i + 1, i) for i in range(n_col - 1)])  2.44 us
  transfers between devices with their start and end apart: 7, of which 2 were waited for; matrix products, arithmetic and copies ran while one was open for 3% of the time, Pallas kernels for 16%

profile of v2, /device:TPU:26, one launch (start us, length us, event | category | flops | bytes accessed | tf_op | source)
XLA Modules:
  0.0 116.6 jit_solution(4927978440458258944)
XLA Ops:
  0.0 1.8 %slice_reduce_fusion.1 = (bf16[18,128]{1,0:T(8,128)(2,1)S(1)}, bf16[18,128]{1,0:T(8,128)(2,1)S(1)}) fusion(bf16[18,128,2048]{2,1,0:T(8,128)(2,1)} %bitcast.8), kind=kLoop, calls=%fused_computation.1 | loop fusion | bytes 18432 | tf_op jit(solution)/shard_map/slice | solution.py:335
  1.8 2.4 %collective-permute-start.2 = (bf16[18,128]{1,0:T(8,128)(2,1)S(1)}, bf16[18,128]{1,0:T(8,128)(2,1)S(1)}, u32[]{:S(2)}, u32[]{:S(2)}) collective-permute-start(bf16[18,128]{1,0:T(8,128)(2,1)S(1)} %get-tuple-element.25), channel_id=1, source_target_pairs={{1,0},{2,1},{3,2},{5,4},{6,5},{7,6},{9,8},{10,9},{11,10},{13,12},{... | collective-permute-start | bytes 13832 | tf_op jit(solution)/shard_map/ppermute | solution.py:339
  4.3 4.3 %collective-permute-start.3 = (bf16[18,128]{1,0:T(8,128)(2,1)S(1)}, bf16[18,128]{1,0:T(8,128)(2,1)S(1)}, u32[]{:S(2)}, u32[]{:S(2)}) collective-permute-start(bf16[18,128]{1,0:T(8,128)(2,1)S(1)} %get-tuple-element.26), channel_id=1, source_target_pairs={{0,1},{1,2},{2,3},{4,5},{5,6},{6,7},{8,9},{9,10},{10,11},{12,13},{... | collective-permute-start | bytes 13832 | tf_op jit(solution)/shard_map/ppermute | solution.py:338
  8.6 1.2 %dynamic-slice_bitcast_fusion = bf16[18,1,2048]{2,1,0:T(2,128)(2,1)S(1)} fusion(bf16[1,18,128,2048]{3,2,1,0:T(8,128)(2,1)} %param.8, s32[]{:T(128)S(6)} %select_n.9), kind=kLoop, calls=%fused_computation.3 | loop fusion | bytes 147460 | tf_op jit(solution)/shard_map/dynamic_slice | solution.py:314
  9.8 0.1 collective-permute-start
  10.6 0.1 pad_add_fusion.info_ref
  10.6 0.8 reshape.6
  11.4 0.8 concatenate.3.param_ref
  12.2 0.0 collective-permute-done.2
  12.2 0.0 collective-permute-done.3
  12.2 0.8 broadcast_select_fusion.rest_0_
  13.0 0.0 collective-permute-done.halo
  13.0 6.8 %march.5 = s16[4,32,1024]{2,1,0:T(8,128)(2,1)S(1)} custom-call(s32[4]{0:T(128)S(1)} %pad_add_fusion.info_ref, f32[27]{0:T(128)S(1)} %concatenate.3.param_ref, bf16[18,128,2048]{2,1,0:T(8,128)(2,1)} %bitcast.9, bf16[18,128,2048]{2,1,0:T(8,128)(2,1)} %bitcast.10, bf16[18,128,2048]{2,1,0:T(8,128)(2,1)} %bitcast.11, bf16[18,128,2048]{2,1,0:T(8,128)(2,1)} %bitcast.12, ...), custom_call_target="tpu_custom_call" | custom-call | tf_op jit(solution)/shard_map/march/pallas_call | solution.py:214
  19.8 11.9 %march.6 = s16[4,32,2048]{2,1,0:T(8,128)(2,1)S(1)} custom-call(s32[4]{0:T(128)S(1)} %pad_add_fusion.info_ref, f32[27]{0:T(128)S(1)} %concatenate.3.param_ref, bf16[18,128,2048]{2,1,0:T(8,128)(2,1)} %bitcast.14, bf16[18,128,2048]{2,1,0:T(8,128)(2,1)} %bitcast.15, bf16[18,128,2048]{2,1,0:T(8,128)(2,1)} %bitcast.16, bf16[18,128,2048]{2,1,0:T(8,128)(2,1)} %bitcast.17, ...), custom_call_target="tpu_custom_call" | custom-call | tf_op jit(solution)/shard_map/march/pallas_call | solution.py:214
  31.7 0.1 collective-permute-start.5
  31.8 1.9 %collective-permute-start.1 = (s16[4,32,1024]{2,1,0:T(8,128)(2,1)S(1)}, s16[4,32,1024]{2,1,0:T(8,128)(2,1)S(1)}, u32[]{:S(2)}, u32[]{:S(2)}) collective-permute-start(s16[4,32,1024]{2,1,0:T(8,128)(2,1)S(1)} %march.5), channel_id=1, source_target_pairs={{0,16},{8,24},{16,0},{24,8},{1,17},{9,25},{17,1},{25,9},{2,18},{10... | collective-permute-start | bytes 786440 | tf_op jit(solution)/shard_map/ppermute | solution.py:349
  33.7 23.5 %collective-permute-done.1.rest_2_ = s16[4,32,1024]{2,1,0:T(8,128)(2,1)S(1)} collective-permute-done((s16[4,32,1024]{2,1,0:T(8,128)(2,1)S(1)}, s16[4,32,1024]{2,1,0:T(8,128)(2,1)S(1)}, u32[]{:S(2)}, u32[]{:S(2)}) %collective-permute-start.1) | collective-permute-done | bytes 262176 | tf_op jit(solution)/shard_map/ppermute | solution.py:349
  57.2 6.9 %march.7 = s16[4,32,1024]{2,1,0:T(8,128)(2,1)S(1)} custom-call(s32[4]{0:T(128)S(1)} %pad_add_fusion.info_ref, f32[27]{0:T(128)S(1)} %concatenate.3.param_ref, bf16[18,128,2048]{2,1,0:T(8,128)(2,1)} %bitcast.20, bf16[18,128,2048]{2,1,0:T(8,128)(2,1)} %bitcast.19, bf16[18,128,2048]{2,1,0:T(8,128)(2,1)} %bitcast.21, bf16[18,128,2048]{2,1,0:T(8,128)(2,1)} %bitcast.22, ...), custom_call_target="tpu_custom_call" | custom-call | tf_op jit(solution)/shard_map/march/pallas_call | solution.py:214
  64.1 0.0 collective-permute-done.5.rest_1_
  64.1 11.8 %march.8 = s16[4,32,2048]{2,1,0:T(8,128)(2,1)S(1)} custom-call(s32[4]{0:T(128)S(1)} %pad_add_fusion.info_ref, f32[27]{0:T(128)S(1)} %concatenate.3.param_ref, bf16[18,128,2048]{2,1,0:T(8,128)(2,1)} %bitcast.24, bf16[18,128,2048]{2,1,0:T(8,128)(2,1)} %bitcast.25, bf16[18,128,2048]{2,1,0:T(8,128)(2,1)} %bitcast.26, bf16[18,128,2048]{2,1,0:T(8,128)(2,1)} %bitcast.27, ...), custom_call_target="tpu_custom_call" | custom-call | tf_op jit(solution)/shard_map/march/pallas_call | solution.py:214
  75.9 0.0 copy-start
  75.9 0.2 collective-permute-start.6
  76.2 2.6 %collective-permute-start.4 = (s16[4,32,1024]{2,1,0:T(8,128)(2,1)S(1)}, s16[4,32,1024]{2,1,0:T(8,128)(2,1)S(1)}, u32[]{:S(2)}, u32[]{:S(2)}) collective-permute-start(s16[4,32,1024]{2,1,0:T(8,128)(2,1)S(1)} %march.7), channel_id=1, source_target_pairs={{0,16},{8,24},{16,0},{24,8},{1,17},{9,25},{17,1},{25,9},{2,18},{10... | collective-permute-start | bytes 786440 | tf_op jit(solution)/shard_map/ppermute | solution.py:349
  78.8 22.8 %collective-permute-done.4.rest_3_ = s16[4,32,1024]{2,1,0:T(8,128)(2,1)S(1)} collective-permute-done((s16[4,32,1024]{2,1,0:T(8,128)(2,1)S(1)}, s16[4,32,1024]{2,1,0:T(8,128)(2,1)S(1)}, u32[]{:S(2)}, u32[]{:S(2)}) %collective-permute-start.4) | collective-permute-done | bytes 262176 | tf_op jit(solution)/shard_map/ppermute | solution.py:349
  101.6 11.6 %march.9.rest_0_ = f32[4,32,2048]{2,1,0:T(8,128)S(1)} custom-call(s32[4]{0:T(128)S(1)} %pad_add_fusion.info_ref, f32[27]{0:T(128)S(1)} %concatenate.3.param_ref, bf16[18,128,2048]{2,1,0:T(8,128)(2,1)} %bitcast.29, bf16[18,128,2048]{2,1,0:T(8,128)(2,1)} %bitcast.30, bf16[18,128,2048]{2,1,0:T(8,128)(2,1)} %bitcast.31, bf16[18,128,2048]{2,1,0:T(8,128)(2,1)} %bitcast.32, ...), custom_call_target="tpu_custom_call" | custom-call | tf_op jit(solution)/shard_map/march/pallas_call | solution.py:214
  113.2 0.0 collective-permute-done.6.rest_4_
  113.3 0.0 copy-done
  113.3 3.3 %composite.1 = f32[4,32,2048]{2,1,0:T(8,128)} custom-call(s32[4]{0:T(128)S(1)} %pad_add_fusion.info_ref, s32[4]{0:T(128)S(1)} %copy-done, f32[4,32,2048]{2,1,0:T(8,128)S(1)} %march.9.rest_0_, s16[4,32,2048]{2,1,0:T(8,128)(2,1)S(1)} %collective-permute-done.5.rest_1_, s16[4,32,1024]{2,1,0:T(8,128)(2,1)S(1)} %collective-permute-done.1.rest_2_, ...), custom_call_target="tpu_custom_call" | custom-call | tf_op jit(solution)/shard_map/composite/pallas_call | solution.py:277
  (1 shorter events, 0.0 us)
Async XLA Ops:
  1.8 10.4 %collective-permute-start.2 = (bf16[18,128]{1,0:T(8,128)(2,1)S(1)}, bf16[18,128]{1,0:T(8,128)(2,1)S(1)}, u32[]{:S(2)}, u32[]{:S(2)}) collective-permute-start(bf16[18,128]{1,0:T(8,128)(2,1)S(1)} %get-tuple-element.25), channel_id=1, source_target_pairs={{1,0},{2,1},{3,2},{5,4},{6,5},{7,6},{9,8},{10,9},{11,10},{13,12},{... | collective-permute-start | bytes 13832 | tf_op jit(solution)/shard_map/ppermute | solution.py:339
  4.3 7.9 %collective-permute-start.3 = (bf16[18,128]{1,0:T(8,128)(2,1)S(1)}, bf16[18,128]{1,0:T(8,128)(2,1)S(1)}, u32[]{:S(2)}, u32[]{:S(2)}) collective-permute-start(bf16[18,128]{1,0:T(8,128)(2,1)S(1)} %get-tuple-element.26), channel_id=1, source_target_pairs={{0,1},{1,2},{2,3},{4,5},{5,6},{6,7},{8,9},{9,10},{10,11},{12,13},{... | collective-permute-start | bytes 13832 | tf_op jit(solution)/shard_map/ppermute | solution.py:338
  9.8 3.2 %collective-permute-start = (bf16[18,1,2048]{2,1,0:T(2,128)(2,1)S(1)}, bf16[18,1,2048]{2,1,0:T(2,128)(2,1)S(1)}, u32[]{:S(2)}, u32[]{:S(2)}) collective-permute-start(bf16[18,1,2048]{2,1,0:T(2,128)(2,1)S(1)} %dynamic-slice_bitcast_fusion), channel_id=1, source_target_pairs={{0,4},{4,0},{1,5},{5,1},{2,6},{6,2},{3,7},{7,3},{8,12},{12,8},{9,1... | collective-permute-start | bytes 221192 | tf_op jit(solution)/shard_map/ppermute | solution.py:315
  31.7 32.4 %collective-permute-start.5 = (s16[4,32,2048]{2,1,0:T(8,128)(2,1)S(1)}, s16[4,32,2048]{2,1,0:T(8,128)(2,1)S(1)}, u32[]{:S(2)}, u32[]{:S(2)}) collective-permute-start(s16[4,32,2048]{2,1,0:T(8,128)(2,1)S(1)} %march.6), channel_id=1, source_target_pairs={{0,8},{8,16},{16,24},{24,0},{1,9},{9,17},{17,25},{25,1},{2,10},{10... | collective-permute-start | bytes 1572872 | tf_op jit(solution)/shard_map/ppermute | solution.py:349
  31.8 25.4 %collective-permute-start.1 = (s16[4,32,1024]{2,1,0:T(8,128)(2,1)S(1)}, s16[4,32,1024]{2,1,0:T(8,128)(2,1)S(1)}, u32[]{:S(2)}, u32[]{:S(2)}) collective-permute-start(s16[4,32,1024]{2,1,0:T(8,128)(2,1)S(1)} %march.5), channel_id=1, source_target_pairs={{0,16},{8,24},{16,0},{24,8},{1,17},{9,25},{17,1},{25,9},{2,18},{10... | collective-permute-start | bytes 786440 | tf_op jit(solution)/shard_map/ppermute | solution.py:349
  75.9 37.3 %copy-start = (s32[4]{0:T(128)S(1)}, s32[4]{0:T(128)}, u32[]{:S(2)}) copy-start(s32[4]{0:T(128)} %order_ref.1) | copy-start | bytes 52
  75.9 37.3 %collective-permute-start.6 = (s16[4,32,2048]{2,1,0:T(8,128)(2,1)S(1)}, s16[4,32,2048]{2,1,0:T(8,128)(2,1)S(1)}, u32[]{:S(2)}, u32[]{:S(2)}) collective-permute-start(s16[4,32,2048]{2,1,0:T(8,128)(2,1)S(1)} %march.8), channel_id=1, source_target_pairs={{0,24},{8,0},{16,8},{24,16},{1,25},{9,1},{17,9},{25,17},{2,26},{10... | collective-permute-start | bytes 1572872 | tf_op jit(solution)/shard_map/ppermute | solution.py:349
  76.2 25.4 %collective-permute-start.4 = (s16[4,32,1024]{2,1,0:T(8,128)(2,1)S(1)}, s16[4,32,1024]{2,1,0:T(8,128)(2,1)S(1)}, u32[]{:S(2)}, u32[]{:S(2)}) collective-permute-start(s16[4,32,1024]{2,1,0:T(8,128)(2,1)S(1)} %march.7), channel_id=1, source_target_pairs={{0,16},{8,24},{16,0},{24,8},{1,17},{9,25},{17,1},{25,9},{2,18},{10... | collective-permute-start | bytes 786440 | tf_op jit(solution)/shard_map/ppermute | solution.py:349

commit v3 on v2

--- a/solution.py
+++ b/solution.py
@@ -13,7 +13,8 @@
 SUB = 8
 GROUP = 2
 EDGES_AFTER = False
-LAG = 2
+LAG = 9
+SPLIT = 1
 STEP = 8
 WIDE = 4
 UNROLL = 2
@@ -290,13 +291,17 @@
 
 
 def plan(parts, all_tiles):
+    far = parts // 2
+    shifts = [far] + [k for k in range(1, parts) if k != far]
     half, quarter = all_tiles // 2, all_tiles // 4
-    far = parts // 2
-    pieces = [(k, 0, all_tiles) for k in range(1, parts) if k != far]
-    pieces.insert(0, (far, quarter, half))
-    pieces.insert(2, (far, quarter + half, half))
-    pieces.append((0, 0, all_tiles))
-    return [(k, at, count, math.gcd(STEP, quarter if k == far else count)) for k, at, count in pieces]
+    pieces = []
+    for turn, k in enumerate(shifts + [0]):
+        if turn < SPLIT and k != 0:
+            pieces.append((turn, k, quarter, half))
+            pieces.append((turn + SPLIT, k, quarter + half, half))
+        else:
+            pieces.append((turn + 2 * SPLIT, k, 0, all_tiles))
+    return [(k, at, count, math.gcd(STEP, quarter if count == half else count)) for turn, k, at, count in sorted(pieces)]
 
 
 def per_device(volume, order, empty, bump_center, bump_width, bump_height, bump_color, light_dir):
@@ -346,6 +351,8 @@
         layer = march(volume, params, info, row_halo, halos, shift, at, count, tiles, bumps, parts)
         marched.append(layer)
         if shift != 0:
+            if turn >= 2:
+                sent[turn - 2], layer = lax.optimization_barrier((sent[turn - 2], layer))
             layer = lax.ppermute(layer, "depth", [(i, (i + shift) % parts) for i in range(parts)])
         pieces[shift].append((at, len(sent)))
         sent.append(layer)

time: 117 us -> 84.4 us (0.72)
  the two profiles are of different devices: /device:TPU:26 before, /device:TPU:2 now
where the time goes in v3:
time: 84.4 us; the launch traced here: 83.9 us
  Pallas kernels  52.2 us (62%)
  starting transfers between devices  13.6 us (16%)
  waiting for transfers between devices  11.8 us (14%)
  local copies, waits for them, and re-layouts  4.6 us (5%)
  other arithmetic  0.86 us (1%)
    pallas_call x5, Pallas kernels, march(): pl.pallas_call(body, out_shape=jax.ShapeDtypeStruct((4, block, count * LA...  49 us
    ppermute x4, waiting for transfers between devices, per_device(): lax.ppermute(layer, 'depth', [(i, (i + shift) % parts) for i in range(par...  11.8 us
    ppermute x4, starting transfers between devices, per_device(): lax.ppermute(layer, 'depth', [(i, (i + shift) % parts) for i in range(par...  6.77 us
    ppermute x1, starting transfers between devices, per_device(): lax.ppermute(ends[0], 'col', [(i, i + 1) for i in range(n_col - 1)])  4.82 us
    pallas_call x1, Pallas kernels, composite(): pl.pallas_call(body, grid_spec=pltpu.PrefetchScalarGridSpec(num_scalar_pr...  3.29 us
    ppermute x1, starting transfers between devices, per_device(): after = lax.ppermute(ends[1], 'col', [(i + 1, i) for i in range(n_col - 1)])  1.92 us
    slice x1, local copies, waits for them, and re-layouts, per_device(): ends = (volume[:, :, cols - 1], volume[:, :, 0])  1.82 us
  transfers between devices with their start and end apart: 7, of which 2 were waited for; matrix products, arithmetic and copies ran while one was open for 4% of the time, Pallas kernels for 50%

profile of v3, /device:TPU:2, one launch (start us, length us, event | category | flops | bytes accessed | tf_op | source)
XLA Modules:
  0.0 83.9 jit_solution(5598811842062696364)
XLA Ops:
  0.0 1.8 %slice_reduce_fusion.1 = (bf16[18,128]{1,0:T(8,128)(2,1)S(1)}, bf16[18,128]{1,0:T(8,128)(2,1)S(1)}) fusion(bf16[18,128,2048]{2,1,0:T(8,128)(2,1)} %bitcast.8), kind=kLoop, calls=%fused_computation.1 | loop fusion | bytes 18432 | tf_op jit(solution)/shard_map/slice | solution.py:340
  1.8 1.9 %collective-permute-start.1 = (bf16[18,128]{1,0:T(8,128)(2,1)S(1)}, bf16[18,128]{1,0:T(8,128)(2,1)S(1)}, u32[]{:S(2)}, u32[]{:S(2)}) collective-permute-start(bf16[18,128]{1,0:T(8,128)(2,1)S(1)} %get-tuple-element.21), channel_id=1, source_target_pairs={{1,0},{2,1},{3,2},{5,4},{6,5},{7,6},{9,8},{10,9},{11,10},{13,12},{... | collective-permute-start | bytes 13832 | tf_op jit(solution)/shard_map/ppermute | solution.py:344
  3.8 4.8 %collective-permute-start.2 = (bf16[18,128]{1,0:T(8,128)(2,1)S(1)}, bf16[18,128]{1,0:T(8,128)(2,1)S(1)}, u32[]{:S(2)}, u32[]{:S(2)}) collective-permute-start(bf16[18,128]{1,0:T(8,128)(2,1)S(1)} %get-tuple-element.22), channel_id=1, source_target_pairs={{0,1},{1,2},{2,3},{4,5},{5,6},{6,7},{8,9},{9,10},{10,11},{12,13},{... | collective-permute-start | bytes 13832 | tf_op jit(solution)/shard_map/ppermute | solution.py:343
  8.6 1.2 %dynamic-slice_bitcast_fusion = bf16[18,1,2048]{2,1,0:T(2,128)(2,1)S(1)} fusion(bf16[1,18,128,2048]{3,2,1,0:T(8,128)(2,1)} %param.8, s32[]{:T(128)S(6)} %select_n.9), kind=kLoop, calls=%fused_computation.3 | loop fusion | bytes 147460 | tf_op jit(solution)/shard_map/dynamic_slice | solution.py:319
  9.8 0.1 collective-permute-start
  10.6 0.1 pad_add_fusion.info_ref
  10.6 0.8 reshape.6
  11.4 0.8 concatenate.3.param_ref
  12.2 0.0 collective-permute-done.1
  12.2 0.0 collective-permute-done.2
  12.2 0.8 broadcast_select_fusion.rest_0_
  13.0 0.0 collective-permute-done.halo
  13.0 6.8 %march.5 = s16[4,32,1024]{2,1,0:T(8,128)(2,1)S(1)} custom-call(s32[4]{0:T(128)S(1)} %pad_add_fusion.info_ref, f32[27]{0:T(128)S(1)} %concatenate.3.param_ref, bf16[18,128,2048]{2,1,0:T(8,128)(2,1)} %bitcast.9, bf16[18,128,2048]{2,1,0:T(8,128)(2,1)} %bitcast.10, bf16[18,128,2048]{2,1,0:T(8,128)(2,1)} %bitcast.11, bf16[18,128,2048]{2,1,0:T(8,128)(2,1)} %bitcast.12, ...), custom_call_target="tpu_custom_call" | custom-call | tf_op jit(solution)/shard_map/march/pallas_call | solution.py:215
  19.8 2.7 %collective-permute-start.3 = (s16[4,32,1024]{2,1,0:T(8,128)(2,1)S(1)}, s16[4,32,1024]{2,1,0:T(8,128)(2,1)S(1)}, u32[]{:S(2)}, u32[]{:S(2)}) collective-permute-start(s16[4,32,1024]{2,1,0:T(8,128)(2,1)S(1)} %march.5), channel_id=1, source_target_pairs={{0,16},{8,24},{16,0},{24,8},{1,17},{9,25},{17,1},{25,9},{2,18},{10... | collective-permute-start | bytes 786440 | tf_op jit(solution)/shard_map/ppermute | solution.py:356
  22.5 6.9 %march.6 = s16[4,32,1024]{2,1,0:T(8,128)(2,1)S(1)} custom-call(s32[4]{0:T(128)S(1)} %pad_add_fusion.info_ref, f32[27]{0:T(128)S(1)} %concatenate.3.param_ref, bf16[18,128,2048]{2,1,0:T(8,128)(2,1)} %bitcast.14, bf16[18,128,2048]{2,1,0:T(8,128)(2,1)} %bitcast.15, bf16[18,128,2048]{2,1,0:T(8,128)(2,1)} %bitcast.16, bf16[18,128,2048]{2,1,0:T(8,128)(2,1)} %bitcast.17, ...), custom_call_target="tpu_custom_call" | custom-call | tf_op jit(solution)/shard_map/march/pallas_call | solution.py:215
  29.4 0.4 collective-permute-start.5
  29.8 11.8 %march.7 = s16[4,32,2048]{2,1,0:T(8,128)(2,1)S(1)} custom-call(s32[4]{0:T(128)S(1)} %pad_add_fusion.info_ref, f32[27]{0:T(128)S(1)} %concatenate.3.param_ref, bf16[18,128,2048]{2,1,0:T(8,128)(2,1)} %bitcast.20, bf16[18,128,2048]{2,1,0:T(8,128)(2,1)} %bitcast.19, bf16[18,128,2048]{2,1,0:T(8,128)(2,1)} %bitcast.21, bf16[18,128,2048]{2,1,0:T(8,128)(2,1)} %bitcast.22, ...), custom_call_target="tpu_custom_call" | custom-call | tf_op jit(solution)/shard_map/march/pallas_call | solution.py:215
  41.6 11.9 %march.8 = s16[4,32,2048]{2,1,0:T(8,128)(2,1)S(1)} custom-call(s32[4]{0:T(128)S(1)} %pad_add_fusion.info_ref, f32[27]{0:T(128)S(1)} %concatenate.3.param_ref, bf16[18,128,2048]{2,1,0:T(8,128)(2,1)} %bitcast.24, bf16[18,128,2048]{2,1,0:T(8,128)(2,1)} %bitcast.25, bf16[18,128,2048]{2,1,0:T(8,128)(2,1)} %bitcast.26, bf16[18,128,2048]{2,1,0:T(8,128)(2,1)} %bitcast.27, ...), custom_call_target="tpu_custom_call" | custom-call | tf_op jit(solution)/shard_map/march/pallas_call | solution.py:215
  53.5 0.0 copy-start
  53.5 0.0 collective-permute-done.3.rest_2_
  53.5 0.0 collective-permute-done.5.rest_3_
  53.5 3.6 %collective-permute-start.6 = (s16[4,32,2048]{2,1,0:T(8,128)(2,1)S(1)}, s16[4,32,2048]{2,1,0:T(8,128)(2,1)S(1)}, u32[]{:S(2)}, u32[]{:S(2)}) collective-permute-start(s16[4,32,2048]{2,1,0:T(8,128)(2,1)S(1)} %march.8), channel_id=1, source_target_pairs={{0,24},{8,0},{16,8},{24,16},{1,25},{9,1},{17,9},{25,17},{2,26},{10... | collective-permute-start | bytes 1572872 | tf_op jit(solution)/shard_map/ppermute | solution.py:356
  57.2 0.0 collective-permute-start.4
  57.2 11.6 %march.9.rest_0_ = f32[4,32,2048]{2,1,0:T(8,128)S(1)} custom-call(s32[4]{0:T(128)S(1)} %pad_add_fusion.info_ref, f32[27]{0:T(128)S(1)} %concatenate.3.param_ref, bf16[18,128,2048]{2,1,0:T(8,128)(2,1)} %bitcast.29, bf16[18,128,2048]{2,1,0:T(8,128)(2,1)} %bitcast.30, bf16[18,128,2048]{2,1,0:T(8,128)(2,1)} %bitcast.31, bf16[18,128,2048]{2,1,0:T(8,128)(2,1)} %bitcast.32, ...), custom_call_target="tpu_custom_call" | custom-call | tf_op jit(solution)/shard_map/march/pallas_call | solution.py:215
  68.8 0.7 collective-permute-done.6.rest_4_
  69.5 11.1 %collective-permute-done.4.rest_1_ = s16[4,32,2048]{2,1,0:T(8,128)(2,1)S(1)} collective-permute-done((s16[4,32,2048]{2,1,0:T(8,128)(2,1)S(1)}, s16[4,32,2048]{2,1,0:T(8,128)(2,1)S(1)}, u32[]{:S(2)}, u32[]{:S(2)}) %collective-permute-start.4) | collective-permute-done | bytes 524320 | tf_op jit(solution)/shard_map/ppermute | solution.py:356
  80.6 0.0 copy-done
  80.6 3.3 %composite.1 = f32[4,32,2048]{2,1,0:T(8,128)} custom-call(s32[4]{0:T(128)S(1)} %pad_add_fusion.info_ref, s32[4]{0:T(128)S(1)} %copy-done, f32[4,32,2048]{2,1,0:T(8,128)S(1)} %march.9.rest_0_, s16[4,32,2048]{2,1,0:T(8,128)(2,1)S(1)} %collective-permute-done.4.rest_1_, s16[4,32,1024]{2,1,0:T(8,128)(2,1)S(1)} %collective-permute-done.3.rest_2_, ...), custom_call_target="tpu_custom_call" | custom-call | tf_op jit(solution)/shard_map/composite/pallas_call | solution.py:278
  (1 shorter events, 0.0 us)
Async XLA Ops:
  1.8 10.4 %collective-permute-start.1 = (bf16[18,128]{1,0:T(8,128)(2,1)S(1)}, bf16[18,128]{1,0:T(8,128)(2,1)S(1)}, u32[]{:S(2)}, u32[]{:S(2)}) collective-permute-start(bf16[18,128]{1,0:T(8,128)(2,1)S(1)} %get-tuple-element.21), channel_id=1, source_target_pairs={{1,0},{2,1},{3,2},{5,4},{6,5},{7,6},{9,8},{10,9},{11,10},{13,12},{... | collective-permute-start | bytes 13832 | tf_op jit(solution)/shard_map/ppermute | solution.py:344
  3.8 8.4 %collective-permute-start.2 = (bf16[18,128]{1,0:T(8,128)(2,1)S(1)}, bf16[18,128]{1,0:T(8,128)(2,1)S(1)}, u32[]{:S(2)}, u32[]{:S(2)}) collective-permute-start(bf16[18,128]{1,0:T(8,128)(2,1)S(1)} %get-tuple-element.22), channel_id=1, source_target_pairs={{0,1},{1,2},{2,3},{4,5},{5,6},{6,7},{8,9},{9,10},{10,11},{12,13},{... | collective-permute-start | bytes 13832 | tf_op jit(solution)/shard_map/ppermute | solution.py:343
  9.8 3.2 %collective-permute-start = (bf16[18,1,2048]{2,1,0:T(2,128)(2,1)S(1)}, bf16[18,1,2048]{2,1,0:T(2,128)(2,1)S(1)}, u32[]{:S(2)}, u32[]{:S(2)}) collective-permute-start(bf16[18,1,2048]{2,1,0:T(2,128)(2,1)S(1)} %dynamic-slice_bitcast_fusion), channel_id=1, source_target_pairs={{0,4},{4,0},{1,5},{5,1},{2,6},{6,2},{3,7},{7,3},{8,12},{12,8},{9,1... | collective-permute-start | bytes 221192 | tf_op jit(solution)/shard_map/ppermute | solution.py:320
  19.8 33.8 %collective-permute-start.3 = (s16[4,32,1024]{2,1,0:T(8,128)(2,1)S(1)}, s16[4,32,1024]{2,1,0:T(8,128)(2,1)S(1)}, u32[]{:S(2)}, u32[]{:S(2)}) collective-permute-start(s16[4,32,1024]{2,1,0:T(8,128)(2,1)S(1)} %march.5), channel_id=1, source_target_pairs={{0,16},{8,24},{16,0},{24,8},{1,17},{9,25},{17,1},{25,9},{2,18},{10... | collective-permute-start | bytes 786440 | tf_op jit(solution)/shard_map/ppermute | solution.py:356
  29.4 24.1 %collective-permute-start.5 = (s16[4,32,1024]{2,1,0:T(8,128)(2,1)S(1)}, s16[4,32,1024]{2,1,0:T(8,128)(2,1)S(1)}, u32[]{:S(2)}, u32[]{:S(2)}) collective-permute-start(s16[4,32,1024]{2,1,0:T(8,128)(2,1)S(1)} %march.6), channel_id=1, source_target_pairs={{0,16},{8,24},{16,0},{24,8},{1,17},{9,25},{17,1},{25,9},{2,18},{10... | collective-permute-start | bytes 786440 | tf_op jit(solution)/shard_map/ppermute | solution.py:356
  53.5 27.1 %copy-start = (s32[4]{0:T(128)S(1)}, s32[4]{0:T(128)}, u32[]{:S(2)}) copy-start(s32[4]{0:T(128)} %order_ref.1) | copy-start | bytes 52
  53.5 15.9 %collective-permute-start.6 = (s16[4,32,2048]{2,1,0:T(8,128)(2,1)S(1)}, s16[4,32,2048]{2,1,0:T(8,128)(2,1)S(1)}, u32[]{:S(2)}, u32[]{:S(2)}) collective-permute-start(s16[4,32,2048]{2,1,0:T(8,128)(2,1)S(1)} %march.8), channel_id=1, source_target_pairs={{0,24},{8,0},{16,8},{24,16},{1,25},{9,1},{17,9},{25,17},{2,26},{10... | collective-permute-start | bytes 1572872 | tf_op jit(solution)/shard_map/ppermute | solution.py:356
  57.2 23.4 %collective-permute-start.4 = (s16[4,32,2048]{2,1,0:T(8,128)(2,1)S(1)}, s16[4,32,2048]{2,1,0:T(8,128)(2,1)S(1)}, u32[]{:S(2)}, u32[]{:S(2)}) collective-permute-start(s16[4,32,2048]{2,1,0:T(8,128)(2,1)S(1)} %march.7), channel_id=1, source_target_pairs={{0,8},{8,16},{16,24},{24,0},{1,9},{9,17},{17,25},{25,1},{2,10},{10... | collective-permute-start | bytes 1572872 | tf_op jit(solution)/shard_map/ppermute | solution.py:356

commit v4 on v3

--- a/solution.py
+++ b/solution.py
@@ -13,7 +13,7 @@
 SUB = 8
 GROUP = 2
 EDGES_AFTER = False
-LAG = 9
+LAG = 3
 SPLIT = 1
 STEP = 8
 WIDE = 4
@@ -346,12 +346,12 @@
             halos = jnp.where(low_half, after[:, :, None], before[:, :, None])
         if turn > 0:
             params, _ = lax.optimization_barrier((params, marched[-1]))
-        if turn >= LAG:
+        if turn == LAG:
             sent[turn - LAG], params = lax.optimization_barrier((sent[turn - LAG], params))
         layer = march(volume, params, info, row_halo, halos, shift, at, count, tiles, bumps, parts)
         marched.append(layer)
         if shift != 0:
-            if turn >= 2:
+            if turn == 3:
                 sent[turn - 2], layer = lax.optimization_barrier((sent[turn - 2], layer))
             layer = lax.ppermute(layer, "depth", [(i, (i + shift) % parts) for i in range(parts)])
         pieces[shift].append((at, len(sent)))

time: 84.4 us -> 73.9 us (0.88)
  the two profiles are of different devices: /device:TPU:2 before, /device:TPU:0 now
where the time goes in v4:
time: 73.9 us; the launch traced here: 72.6 us
  Pallas kernels  52.3 us (71%)
  starting transfers between devices  10.6 us (14%)
  local copies, waits for them, and re-layouts  4.6 us (6%)
  waiting for transfers between devices  3.56 us (5%)
  other arithmetic  0.84 us (1%)
  between operations  0.8 us (1%)
    pallas_call x5, Pallas kernels, march(): pl.pallas_call(body, out_shape=jax.ShapeDtypeStruct((4, block, count * LA...  49 us
    ppermute x1, starting transfers between devices, per_device(): lax.ppermute(ends[0], 'col', [(i, i + 1) for i in range(n_col - 1)])  5.47 us
    ppermute x4, starting transfers between devices, per_device(): lax.ppermute(layer, 'depth', [(i, (i + shift) % parts) for i in range(par...  3.74 us
    ppermute x4, waiting for transfers between devices, per_device(): lax.ppermute(layer, 'depth', [(i, (i + shift) % parts) for i in range(par...  3.55 us
    pallas_call x1, Pallas kernels, composite(): pl.pallas_call(body, grid_spec=pltpu.PrefetchScalarGridSpec(num_scalar_pr...  3.29 us
    slice x1, local copies, waits for them, and re-layouts, per_device(): ends = (volume[:, :, cols - 1], volume[:, :, 0])  1.82 us
  transfers between devices with their start and end apart: 7, of which 1 were waited for; matrix products, arithmetic and copies ran while one was open for 5% of the time, Pallas kernels for 67%

profile of v4, /device:TPU:0, one launch (start us, length us, event | category | flops | bytes accessed | tf_op | source)
XLA Modules:
  0.0 72.6 jit_solution(16856708701081816374)
XLA Ops:
  0.0 1.8 %slice_reduce_fusion.1 = (bf16[18,128]{1,0:T(8,128)(2,1)S(1)}, bf16[18,128]{1,0:T(8,128)(2,1)S(1)}) fusion(bf16[18,128,2048]{2,1,0:T(8,128)(2,1)} %bitcast.8), kind=kLoop, calls=%fused_computation.1 | loop fusion | bytes 18432 | tf_op jit(solution)/shard_map/slice | solution.py:340
  1.8 1.3 %collective-permute-start.2 = (bf16[18,128]{1,0:T(8,128)(2,1)S(1)}, bf16[18,128]{1,0:T(8,128)(2,1)S(1)}, u32[]{:S(2)}, u32[]{:S(2)}) collective-permute-start(bf16[18,128]{1,0:T(8,128)(2,1)S(1)} %get-tuple-element.21), channel_id=1, source_target_pairs={{1,0},{2,1},{3,2},{5,4},{6,5},{7,6},{9,8},{10,9},{11,10},{13,12},{... | collective-permute-start | bytes 13832 | tf_op jit(solution)/shard_map/ppermute | solution.py:344
  3.1 5.5 %collective-permute-start.3 = (bf16[18,128]{1,0:T(8,128)(2,1)S(1)}, bf16[18,128]{1,0:T(8,128)(2,1)S(1)}, u32[]{:S(2)}, u32[]{:S(2)}) collective-permute-start(bf16[18,128]{1,0:T(8,128)(2,1)S(1)} %get-tuple-element.22), channel_id=1, source_target_pairs={{0,1},{1,2},{2,3},{4,5},{5,6},{6,7},{8,9},{9,10},{10,11},{12,13},{... | collective-permute-start | bytes 13832 | tf_op jit(solution)/shard_map/ppermute | solution.py:343
  8.6 1.2 %dynamic-slice_bitcast_fusion = bf16[18,1,2048]{2,1,0:T(2,128)(2,1)S(1)} fusion(bf16[1,18,128,2048]{3,2,1,0:T(8,128)(2,1)} %param.8, s32[]{:T(128)S(6)} %select_n.9), kind=kLoop, calls=%fused_computation.3 | loop fusion | bytes 147460 | tf_op jit(solution)/shard_map/dynamic_slice | solution.py:319
  9.8 0.1 collective-permute-start
  10.6 0.1 pad_add_fusion.info_ref
  10.7 0.8 %reshape.6 = f32[12]{0:T(128)S(1)} reshape(f32[3,4]{1,0:T(4,128)} %param.14) | data formatting | bytes 96 | tf_op jit(solution)/shard_map/reshape | solution.py:329
  11.4 0.8 %concatenate.3.param_ref = f32[27]{0:T(128)S(1)} concatenate(f32[4]{0:T(128)} %param.11, f32[4]{0:T(128)} %param.12, f32[4]{0:T(128)} %param.13, f32[12]{0:T(128)S(1)} %reshape.6, f32[3]{0:T(128)} %param.15), dimensions={0} | concatenate | bytes 216 | tf_op jit(solution)/shard_map/concatenate | solution.py:329
  12.2 0.0 collective-permute-done.halo
  12.2 6.8 %march.5 = s16[4,32,1024]{2,1,0:T(8,128)(2,1)S(1)} custom-call(s32[4]{0:T(128)S(1)} %pad_add_fusion.info_ref, f32[27]{0:T(128)S(1)} %concatenate.3.param_ref, bf16[18,128,2048]{2,1,0:T(8,128)(2,1)} %bitcast.9, bf16[18,128,2048]{2,1,0:T(8,128)(2,1)} %bitcast.10, bf16[18,128,2048]{2,1,0:T(8,128)(2,1)} %bitcast.11, bf16[18,128,2048]{2,1,0:T(8,128)(2,1)} %bitcast.12, ...), custom_call_target="tpu_custom_call" | custom-call | tf_op jit(solution)/shard_map/march/pallas_call | solution.py:215
  19.0 3.2 %collective-permute-start.1 = (s16[4,32,1024]{2,1,0:T(8,128)(2,1)S(1)}, s16[4,32,1024]{2,1,0:T(8,128)(2,1)S(1)}, u32[]{:S(2)}, u32[]{:S(2)}) collective-permute-start(s16[4,32,1024]{2,1,0:T(8,128)(2,1)S(1)} %march.5), channel_id=1, source_target_pairs={{0,16},{8,24},{16,0},{24,8},{1,17},{9,25},{17,1},{25,9},{2,18},{10... | collective-permute-start | bytes 786440 | tf_op jit(solution)/shard_map/ppermute | solution.py:356
  22.2 0.0 collective-permute-done.2
  22.2 0.0 collective-permute-done.3
  22.2 0.8 %broadcast_select_fusion.rest_0_ = bf16[18,128,128]{2,1,0:T(8,128)(2,1)S(1)} fusion(pred[128]{0:T(512)(128)(4,1)S(1)} %iota_compare_fusion, bf16[18,128]{1,0:T(8,128)(2,1)S(1)} %collective-permute-done.3, bf16[18,128]{1,0:T(8,128)(2,1)S(1)} %collective-permute-done.2), kind=kLoop, calls=%fused_computation.2 | loop fusion | flops 294912 | bytes 599168 | tf_op jit(solution)/shard_map/jit(_where)/select_n | solution.py:346
  23.0 6.9 %march.6 = s16[4,32,1024]{2,1,0:T(8,128)(2,1)S(1)} custom-call(s32[4]{0:T(128)S(1)} %pad_add_fusion.info_ref, f32[27]{0:T(128)S(1)} %concatenate.3.param_ref, bf16[18,128,2048]{2,1,0:T(8,128)(2,1)} %bitcast.14, bf16[18,128,2048]{2,1,0:T(8,128)(2,1)} %bitcast.15, bf16[18,128,2048]{2,1,0:T(8,128)(2,1)} %bitcast.16, bf16[18,128,2048]{2,1,0:T(8,128)(2,1)} %bitcast.17, ...), custom_call_target="tpu_custom_call" | custom-call | tf_op jit(solution)/shard_map/march/pallas_call | solution.py:215
  29.9 0.2 collective-permute-start.5
  30.1 11.8 %march.7 = s16[4,32,2048]{2,1,0:T(8,128)(2,1)S(1)} custom-call(s32[4]{0:T(128)S(1)} %pad_add_fusion.info_ref, f32[27]{0:T(128)S(1)} %concatenate.3.param_ref, bf16[18,128,2048]{2,1,0:T(8,128)(2,1)} %bitcast.20, bf16[18,128,2048]{2,1,0:T(8,128)(2,1)} %bitcast.19, bf16[18,128,2048]{2,1,0:T(8,128)(2,1)} %bitcast.21, bf16[18,128,2048]{2,1,0:T(8,128)(2,1)} %bitcast.22, ...), custom_call_target="tpu_custom_call" | custom-call | tf_op jit(solution)/shard_map/march/pallas_call | solution.py:215
  41.9 0.1 collective-permute-start.4
  42.0 0.0 collective-permute-done.1.rest_2_
  42.0 11.9 %march.8 = s16[4,32,2048]{2,1,0:T(8,128)(2,1)S(1)} custom-call(s32[4]{0:T(128)S(1)} %pad_add_fusion.info_ref, f32[27]{0:T(128)S(1)} %concatenate.3.param_ref, bf16[18,128,2048]{2,1,0:T(8,128)(2,1)} %bitcast.24, bf16[18,128,2048]{2,1,0:T(8,128)(2,1)} %bitcast.25, bf16[18,128,2048]{2,1,0:T(8,128)(2,1)} %bitcast.26, bf16[18,128,2048]{2,1,0:T(8,128)(2,1)} %bitcast.27, ...), custom_call_target="tpu_custom_call" | custom-call | tf_op jit(solution)/shard_map/march/pallas_call | solution.py:215
  53.9 0.0 copy-start
  53.9 0.0 collective-permute-done.5.rest_3_
  53.9 0.2 collective-permute-start.6
  54.1 11.6 %march.9.rest_0_ = f32[4,32,2048]{2,1,0:T(8,128)S(1)} custom-call(s32[4]{0:T(128)S(1)} %pad_add_fusion.info_ref, f32[27]{0:T(128)S(1)} %concatenate.3.param_ref, bf16[18,128,2048]{2,1,0:T(8,128)(2,1)} %bitcast.29, bf16[18,128,2048]{2,1,0:T(8,128)(2,1)} %bitcast.30, bf16[18,128,2048]{2,1,0:T(8,128)(2,1)} %bitcast.31, bf16[18,128,2048]{2,1,0:T(8,128)(2,1)} %bitcast.32, ...), custom_call_target="tpu_custom_call" | custom-call | tf_op jit(solution)/shard_map/march/pallas_call | solution.py:215
  65.8 0.0 collective-permute-done.4.rest_1_
  65.8 3.5 %collective-permute-done.6.rest_4_ = s16[4,32,2048]{2,1,0:T(8,128)(2,1)S(1)} collective-permute-done((s16[4,32,2048]{2,1,0:T(8,128)(2,1)S(1)}, s16[4,32,2048]{2,1,0:T(8,128)(2,1)S(1)}, u32[]{:S(2)}, u32[]{:S(2)}) %collective-permute-start.6) | collective-permute-done | bytes 524320 | tf_op jit(solution)/shard_map/ppermute | solution.py:356
  69.3 0.0 copy-done
  69.3 3.3 %composite.1 = f32[4,32,2048]{2,1,0:T(8,128)} custom-call(s32[4]{0:T(128)S(1)} %pad_add_fusion.info_ref, s32[4]{0:T(128)S(1)} %copy-done, f32[4,32,2048]{2,1,0:T(8,128)S(1)} %march.9.rest_0_, s16[4,32,2048]{2,1,0:T(8,128)(2,1)S(1)} %collective-permute-done.4.rest_1_, s16[4,32,1024]{2,1,0:T(8,128)(2,1)S(1)} %collective-permute-done.1.rest_2_, ...), custom_call_target="tpu_custom_call" | custom-call | tf_op jit(solution)/shard_map/composite/pallas_call | solution.py:278
  (1 shorter events, 0.0 us)
Async XLA Ops:
  1.8 20.4 %collective-permute-start.2 = (bf16[18,128]{1,0:T(8,128)(2,1)S(1)}, bf16[18,128]{1,0:T(8,128)(2,1)S(1)}, u32[]{:S(2)}, u32[]{:S(2)}) collective-permute-start(bf16[18,128]{1,0:T(8,128)(2,1)S(1)} %get-tuple-element.21), channel_id=1, source_target_pairs={{1,0},{2,1},{3,2},{5,4},{6,5},{7,6},{9,8},{10,9},{11,10},{13,12},{... | collective-permute-start | bytes 13832 | tf_op jit(solution)/shard_map/ppermute | solution.py:344
  3.1 19.1 %collective-permute-start.3 = (bf16[18,128]{1,0:T(8,128)(2,1)S(1)}, bf16[18,128]{1,0:T(8,128)(2,1)S(1)}, u32[]{:S(2)}, u32[]{:S(2)}) collective-permute-start(bf16[18,128]{1,0:T(8,128)(2,1)S(1)} %get-tuple-element.22), channel_id=1, source_target_pairs={{0,1},{1,2},{2,3},{4,5},{5,6},{6,7},{8,9},{9,10},{10,11},{12,13},{... | collective-permute-start | bytes 13832 | tf_op jit(solution)/shard_map/ppermute | solution.py:343
  9.8 2.4 %collective-permute-start = (bf16[18,1,2048]{2,1,0:T(2,128)(2,1)S(1)}, bf16[18,1,2048]{2,1,0:T(2,128)(2,1)S(1)}, u32[]{:S(2)}, u32[]{:S(2)}) collective-permute-start(bf16[18,1,2048]{2,1,0:T(2,128)(2,1)S(1)} %dynamic-slice_bitcast_fusion), channel_id=1, source_target_pairs={{0,4},{4,0},{1,5},{5,1},{2,6},{6,2},{3,7},{7,3},{8,12},{12,8},{9,1... | collective-permute-start | bytes 221192 | tf_op jit(solution)/shard_map/ppermute | solution.py:320
  19.0 23.0 %collective-permute-start.1 = (s16[4,32,1024]{2,1,0:T(8,128)(2,1)S(1)}, s16[4,32,1024]{2,1,0:T(8,128)(2,1)S(1)}, u32[]{:S(2)}, u32[]{:S(2)}) collective-permute-start(s16[4,32,1024]{2,1,0:T(8,128)(2,1)S(1)} %march.5), channel_id=1, source_target_pairs={{0,16},{8,24},{16,0},{24,8},{1,17},{9,25},{17,1},{25,9},{2,18},{10... | collective-permute-start | bytes 786440 | tf_op jit(solution)/shard_map/ppermute | solution.py:356
  29.9 24.0 %collective-permute-start.5 = (s16[4,32,1024]{2,1,0:T(8,128)(2,1)S(1)}, s16[4,32,1024]{2,1,0:T(8,128)(2,1)S(1)}, u32[]{:S(2)}, u32[]{:S(2)}) collective-permute-start(s16[4,32,1024]{2,1,0:T(8,128)(2,1)S(1)} %march.6), channel_id=1, source_target_pairs={{0,16},{8,24},{16,0},{24,8},{1,17},{9,25},{17,1},{25,9},{2,18},{10... | collective-permute-start | bytes 786440 | tf_op jit(solution)/shard_map/ppermute | solution.py:356
  41.9 23.9 %collective-permute-start.4 = (s16[4,32,2048]{2,1,0:T(8,128)(2,1)S(1)}, s16[4,32,2048]{2,1,0:T(8,128)(2,1)S(1)}, u32[]{:S(2)}, u32[]{:S(2)}) collective-permute-start(s16[4,32,2048]{2,1,0:T(8,128)(2,1)S(1)} %march.7), channel_id=1, source_target_pairs={{0,8},{8,16},{16,24},{24,0},{1,9},{9,17},{17,25},{25,1},{2,10},{10... | collective-permute-start | bytes 1572872 | tf_op jit(solution)/shard_map/ppermute | solution.py:356
  53.9 15.5 %copy-start = (s32[4]{0:T(128)S(1)}, s32[4]{0:T(128)}, u32[]{:S(2)}) copy-start(s32[4]{0:T(128)} %order_ref.1) | copy-start | bytes 52
  53.9 15.4 %collective-permute-start.6 = (s16[4,32,2048]{2,1,0:T(8,128)(2,1)S(1)}, s16[4,32,2048]{2,1,0:T(8,128)(2,1)S(1)}, u32[]{:S(2)}, u32[]{:S(2)}) collective-permute-start(s16[4,32,2048]{2,1,0:T(8,128)(2,1)S(1)} %march.8), channel_id=1, source_target_pairs={{0,24},{8,0},{16,8},{24,16},{1,25},{9,1},{17,9},{25,17},{2,26},{10... | collective-permute-start | bytes 1572872 | tf_op jit(solution)/shard_map/ppermute | solution.py:356
